TPU v7x, 128 devices: a whole 4x4x4 slice. The times are simulated.
128 devices in a mesh: tm: 16 (over y, z_lo, core), tensor: 8 (over z_hi, x).
Axes of the slice: x: 4, y: 4, z: 4 (z_hi: 2, z_lo: 2; z = z_hi * 2 + z_lo), core: 2. Of those that a mesh axis runs over, the one named last changes fastest.
Arguments:
- activations: bfloat16 [16384, 3072], P(('tm', 'tensor')), may hold values from -6 to 6
- mod_gain: float32 [3072], replicated, may hold values from 0.1 to 1.9
- mod_shift: float32 [3072], replicated, may hold values from -3 to 3
- out_gate: float32 [3072], replicated, may hold values from 0.5 to 2
- qkv_weight: bfloat16 [3072, 24, 384], P(None, 'tensor'), may hold values from -0.109375 to 0.109375
- out_weight: bfloat16 [24, 128, 3072], P('tensor'), may hold values from -0.109375 to 0.109375
- tile_mask: int32 [64, 7, 4, 4], P('tm'), may hold values 0 or 1
- cotangent: bfloat16 [16384, 3072], P('tm'), may hold values from -6 to 6
Outputs:
- layer_out: bfloat16 [16384, 3072], P(('tm', 'tensor'))
- input_grad: bfloat16 [16384, 3072], P(('tm', 'tensor'))
All inputs are finite; a program needn't handle non-finite values. No bound on the sum of `tile_mask` on one device may be relied on, other than what follows from the above.
Results may differ from a plain program's by a relative error of at most 0.015.
Values may be sent and summed in bfloat16 or wider, within the bound.
A program may use at most 320 MiB of HBM per device.

v0:
```python
import jax
import jax.numpy as jnp
from jax import lax
from jax.sharding import PartitionSpec as P

FRAME = 256
TILE = 64
RADIUS = 3


EPSILON = 1e-06


def extended(cells, sides, width):
    for axis, dim in sides:
        count = lax.axis_size(axis)
        ends = count - 1
        head = lax.slice_in_dim(cells, 0, width, axis=dim)
        tail = lax.slice_in_dim(cells, cells.shape[dim] - width, cells.shape[dim], axis=dim)
        cells = jnp.concatenate(
            [
                lax.ppermute(tail, axis, [(i, (i + 1) % count) for i in range(ends)]),
                cells,
                lax.ppermute(head, axis, [((i + 1) % count, i) for i in range(ends)]),
            ],
            axis=dim,
        )
    return cells


def norm_rows(inputs, mod_gain, mod_shift):
    floated = inputs.astype(jnp.float32)
    row_mean = jnp.mean(floated, axis=-1, keepdims=True)
    centered = floated - row_mean
    inverse = lax.rsqrt(jnp.mean(centered * centered, axis=-1, keepdims=True) + EPSILON)
    standard = centered * inverse
    return (standard, inverse, (standard * mod_gain + mod_shift).astype(jnp.bfloat16))


def norm_back(grad_norm, standard, inverse, mod_gain, cotangent):
    scaled_grad = grad_norm * mod_gain
    centered = scaled_grad - jnp.mean(scaled_grad, axis=-1, keepdims=True)
    projected = standard * jnp.mean(scaled_grad * standard, axis=-1, keepdims=True)
    return (cotangent.astype(jnp.float32) + inverse * (centered - projected)).astype(jnp.bfloat16)


def window_mask(tile_mask, first_frame, total_frames):
    expanded = jnp.repeat(jnp.repeat(tile_mask, TILE, axis=2), TILE, axis=3)
    frame_ids = lax.broadcasted_iota(jnp.int32, expanded.shape, 0) + first_frame
    offset_ids = lax.broadcasted_iota(jnp.int32, expanded.shape, 1)
    query_pos = lax.broadcasted_iota(jnp.int32, expanded.shape, 2)
    key_pos = lax.broadcasted_iota(jnp.int32, expanded.shape, 3)
    source = frame_ids + offset_ids - RADIUS
    diagonal = (offset_ids == RADIUS) & (query_pos // TILE == key_pos // TILE)
    inside = (source >= 0) & (source < total_frames)
    allowed = ((expanded == 1) | diagonal) & inside
    return jnp.transpose(allowed, (0, 2, 1, 3)).reshape(expanded.shape[0], expanded.shape[2], -1)


def window_rows(padded, frame_count, radius):
    stacked = jnp.stack(
        [padded[offset : offset + frame_count] for offset in range(2 * radius + 1)], axis=1
    )
    return stacked.reshape(frame_count, -1, padded.shape[2], padded.shape[3])


def spread_windows(window_grads, frame_count, radius):
    by_offset = window_grads.reshape(
        frame_count, 2 * radius + 1, -1, window_grads.shape[2], window_grads.shape[3]
    )
    summed = jnp.zeros((frame_count + 2 * radius,) + by_offset.shape[2:], jnp.float32)
    for offset in range(2 * radius + 1):
        summed = summed + jnp.pad(
            by_offset[:, offset], ((offset, 2 * radius - offset), (0, 0), (0, 0), (0, 0))
        )
    return summed


def attend(queries, window, allowed, score_scale):
    head_dim = queries.shape[-1]
    key_rows = window[..., :head_dim]
    value_rows = window[..., head_dim:]
    scores = (
        jnp.einsum("fqhc,fkhc->fhqk", queries, key_rows, preferred_element_type=jnp.float32)
        * score_scale
    )
    exponent = jnp.where(allowed[:, None], jnp.exp(scores), 0.0)
    totals = jnp.sum(exponent, axis=-1)
    numerator = jnp.einsum(
        "fhqk,fkhc->fqhc",
        exponent.astype(jnp.bfloat16),
        value_rows,
        preferred_element_type=jnp.float32,
    )
    output = (numerator / jnp.transpose(totals, (0, 2, 1))[..., None]).astype(jnp.bfloat16)
    return (output, totals)


def attend_back(queries, window, allowed, totals, output, grad_out, score_scale):
    head_dim = queries.shape[-1]
    key_rows = window[..., :head_dim]
    value_rows = window[..., head_dim:]
    scores = (
        jnp.einsum("fqhc,fkhc->fhqk", queries, key_rows, preferred_element_type=jnp.float32)
        * score_scale
    )
    probability = jnp.where(allowed[:, None], jnp.exp(scores), 0.0) / totals[..., None]
    grad_values = jnp.einsum(
        "fhqk,fqhc->fkhc",
        probability.astype(jnp.bfloat16),
        grad_out,
        preferred_element_type=jnp.float32,
    )
    grad_probs = jnp.einsum(
        "fqhc,fkhc->fhqk", grad_out, value_rows, preferred_element_type=jnp.float32
    )
    row_delta = jnp.einsum("fqhc,fqhc->fhq", grad_out, output, preferred_element_type=jnp.float32)
    grad_scores = (probability * (grad_probs - row_delta[..., None])).astype(jnp.bfloat16)
    grad_queries = jnp.einsum(
        "fhqk,fkhc->fqhc", grad_scores, key_rows, preferred_element_type=jnp.float32
    )
    grad_queries = (grad_queries * score_scale).astype(jnp.bfloat16)
    grad_keys = (
        jnp.einsum("fhqk,fqhc->fkhc", grad_scores, queries, preferred_element_type=jnp.float32)
        * score_scale
    )
    return (grad_queries, jnp.concatenate([grad_keys, grad_values], axis=-1))


def on_device(
    activations, mod_gain, mod_shift, out_gate, qkv_weight, out_weight, tile_mask, cotangent
):
    shard_rows = activations.shape[0]
    frame_count = tile_mask.shape[0]
    heads_here = qkv_weight.shape[1]
    head_dim = out_weight.shape[1]
    group_rows = frame_count * FRAME
    score_scale = head_dim ** (-0.5)
    standard, inverse, modulated = norm_rows(activations, mod_gain, mod_shift)
    joined_qkv = jnp.einsum(
        "rd,dhc->rhc",
        lax.all_gather(modulated, "tensor", axis=0, tiled=True),
        qkv_weight,
        preferred_element_type=jnp.float32,
    ).astype(jnp.bfloat16)
    joined_qkv = joined_qkv.reshape(frame_count, FRAME, heads_here, 3 * head_dim)
    queries = joined_qkv[..., :head_dim]
    padded = extended(joined_qkv[..., head_dim:], (("tm", 0),), RADIUS)
    first_frame = lax.axis_index("tm") * frame_count
    allowed = window_mask(tile_mask, first_frame, frame_count * lax.axis_size("tm"))
    window = window_rows(padded, frame_count, RADIUS)
    output, totals = attend(queries, window, allowed, score_scale)
    flat_out = output.reshape(group_rows, heads_here, head_dim)
    row_block = flat_out
    projection = lax.psum_scatter(
        jnp.einsum("rhc,hcd->rd", row_block, out_weight, preferred_element_type=jnp.float32).astype(
            jnp.bfloat16
        ),
        "tensor",
        scatter_dimension=0,
        tiled=True,
    ).astype(jnp.float32)
    layer_out = (activations.astype(jnp.float32) + out_gate * projection).astype(jnp.bfloat16)
    scaled = (cotangent.astype(jnp.float32) * out_gate).astype(jnp.bfloat16)
    grad_out = jnp.einsum("rd,hcd->rhc", scaled, out_weight, preferred_element_type=jnp.float32)
    grad_out = grad_out.astype(jnp.bfloat16).reshape(frame_count, FRAME, heads_here, head_dim)
    grad_queries, window_grads = attend_back(
        queries, window, allowed, totals, output, grad_out, score_scale
    )
    spread = spread_windows(window_grads, frame_count, RADIUS)
    rim_frames = jnp.concatenate([spread[:RADIUS], spread[frame_count + RADIUS :]], axis=0)
    arrived = extended(rim_frames.astype(jnp.bfloat16), (("tm", 0),), RADIUS).astype(
        rim_frames.dtype
    )
    own_part = spread[RADIUS : frame_count + RADIUS]
    from_below = jnp.pad(arrived[:RADIUS], ((0, frame_count - RADIUS), (0, 0), (0, 0), (0, 0)))
    from_above = jnp.pad(arrived[3 * RADIUS :], ((frame_count - RADIUS, 0), (0, 0), (0, 0), (0, 0)))
    grad_pairs = (own_part + from_below + from_above).astype(jnp.bfloat16)
    grad_joined = jnp.concatenate([grad_queries, grad_pairs], axis=-1).reshape(
        group_rows, heads_here, 3 * head_dim
    )
    row_block = grad_joined
    grad_norm = lax.psum_scatter(
        jnp.einsum("rhc,dhc->rd", row_block, qkv_weight, preferred_element_type=jnp.float32).astype(
            jnp.bfloat16
        ),
        "tensor",
        scatter_dimension=0,
        tiled=True,
    ).astype(jnp.float32)
    own_cotangent = lax.dynamic_slice_in_dim(
        cotangent, lax.axis_index("tensor") * shard_rows, shard_rows, 0
    )
    input_grad = norm_back(grad_norm, standard, inverse, mod_gain, own_cotangent)
    return (layer_out, input_grad)


def solution(mesh):
    placed = (
        P(("tm", "tensor"), None),
        P(),
        P(),
        P(),
        P(None, "tensor", None),
        P("tensor", None, None),
        P("tm", None, None, None),
        P("tm", None),
    )
    return jax.shard_map(
        on_device,
        mesh=mesh,
        in_specs=placed,
        out_specs=(P(("tm", "tensor"), None), P(("tm", "tensor"), None)),
        check_vma=False,
    )
```

profile of v0, /device:TPU:17, one launch (start us, length us, event | category | flops | bytes accessed | tf_op | source)
XLA Modules:
  0.0 537.4 jit_solution(2131804124469288829)
XLA Ops:
  7.2 0.0 copy-start
  7.2 0.0 all-gather.2.cloned.1.call-start
  7.2 1.5 convert_reduce_fusion
  8.7 1.5 fusion.50
  10.2 0.5 copy-done.16
  10.8 2.4 fusion.44
  13.2 0.0 all-gather.2.cloned.1.call-update
  13.2 0.0 reduce-scatter.5.cloned.1.call-start
  13.3 0.2 copy.26
  13.5 0.2 broadcast_in_dim.36
  13.7 0.8 eq.23
  14.4 90.4 %all-gather.2.cloned.1.call-done = bf16[1024,3072]{1,0:T(8,128)(2,1)} async-done(((bf16[128,3072]{1,0:T(8,128)(2,1)}), bf16[1024,3072]{1,0:T(8,128)(2,1)}) %all-gather.2.cloned.1.call-update) | async-done | bytes 6291472 | tf_op jit(solution)/shard_map/all_gather | solution.py:142
  104.8 12.4 %fusion.35 = bf16[1024,3,384]{2,0,1:T(8,128)(2,1)S(1)} fusion(bf16[3072,3,384]{2,0,1:T(8,128)(2,1)} %param.12, bf16[1024,3072]{1,0:T(8,128)(2,1)} %all-gather.2.cloned.1.call-done), kind=kOutput, calls=%fused_computation.60 | convolution fusion | flops 7248936960 | bytes 15728640 | tf_op jit(solution)/shard_map/rd,dhc->rhc/dot_general | solution.py:140
  117.3 1.8 fusion.93
  119.1 3.4 collective-permute-start
  122.5 6.3 %fusion.74 = bf16[1024,3,128]{2,0,1:T(8,128)(2,1)} fusion(bf16[3,128,3072]{2,1,0:T(8,128)(2,1)S(1)} %copy-done, bf16[1024,3072]{1,0:T(8,128)(2,1)} %param.15, f32[3072]{0:T(1024)S(1)} %copy-done.12), kind=kOutput, calls=%fused_computation.100 | convolution fusion | flops 2425749504 | bytes 9449472 | tf_op jit(solution)/shard_map/rd,hcd->rhc/dot_general | solution.py:165
  128.8 1.9 collective-permute-start.1
  130.8 4.6 fusion.15
  135.3 5.5 %copy.27 = pred[4,256,1792]{2,1,0:T(8,128)(4,1)} copy(pred[4,256,1792]{1,2,0:T(8,128)(4,1)} %bitcast.112) | data formatting | bytes 3670016 | tf_op jit(solution)/shard_map/jit(_where)/broadcast_in_dim | solution.py:87
  140.8 2.6 copy.50
  143.4 1.5 slice.112
  144.9 3.7 collective-permute-done
  148.6 1.4 fusion.63
  150.0 1.3 fusion.60
  151.3 1.3 fusion.67
  152.5 0.5 copy-done.3
  153.0 0.1 bitcast_dynamic-update-slice_fusion
  153.2 0.1 fusion.57
  153.3 0.1 fusion.54
  153.4 0.1 fusion.65
  153.5 4.8 copy.25
  158.3 13.4 %fusion.1 = (f32[4,3,256]{2,1,0:T(4,128)S(1)}, f32[4,3,256,1792]{3,2,1,0:T(8,128)}) fusion(pred[4,256,1792]{2,1,0:T(8,128)(4,1)S(1)} %copy-done.6, bf16[4,1792,3,256]{3,1,2,0:T(8,128)(2,1)} %bitcast.108, bf16[4,256,3,384]{3,1,0,2:T(8,128)(2,1)S(1)} %bitcast.107), kind=kOutput, calls=%fused_computation.4 | convolution fusion | flops 1425798144 | bytes 30158848 | tf_op jit(solution)/shard_map/fqhc,fkhc->fhqk/dot_general | solution.py:84
  171.7 12.9 %fusion.22 = f32[4,1792,3,128]{1,3,2,0:T(8,128)} fusion(f32[4,3,256,1792]{3,2,1,0:T(8,128)} %get-tuple-element.20, f32[4,3,256]{2,1,0:T(4,128)S(1)} %get-tuple-element.19, pred[4,256,1792]{2,1,0:T(8,128)(4,1)S(1)} %copy-done.6, bf16[4,256,3,128]{3,1,0,2:T(8,128)(2,1)S(1)} %bitcast.116), kind=kOutput, calls=%fused_computation.30 | convolution fusion | flops 1431306240 | bytes 35663872 | tf_op jit(solution)/shard_map/fhqk,fqhc->fkhc/dot_general | solution.py:108
  184.6 13.6 %multiply_reduce_fusion = (f32[4,3,256]{2,1,0:T(4,128)S(1)}, bf16[4,256,3,128]{1,3,2,0:T(8,128)(2,1)}) fusion(f32[4,3,256,128]{2,3,1,0:T(8,128)} %copy.50, f32[4,256,3]{1,2,0:T(4,128)S(1)} %bitcast.120, f32[4,3,256,1792]{3,2,1,0:T(8,128)} %get-tuple-element.20, pred[4,256,1792]{2,1,0:T(8,128)(4,1)} %copy.27, bf16[4,1792,3,256]{3,1,2,0:T(8,128)(2,1)} %bitcast.109), kind=kOutput, calls=%fused_computation.96 | convolution fusion | flops 1427764224 | bytes 31744000 | tf_op jit(solution)/shard_map/fhqk,fkhc->fqhc/dot_general | solution.py:89
  198.2 17.3 %multiply_convert_fusion = bf16[4,3,256,1792]{3,2,1,0:T(8,128)(2,1)} fusion(f32[4,3,256]{2,1,0:T(4,128)S(1)} %get-tuple-element.21, bf16[4,1792,3,256]{3,1,2,0:T(8,128)(2,1)} %bitcast.110, f32[4,3,256]{2,1,0:T(4,128)S(1)} %get-tuple-element.19, f32[4,3,256,1792]{3,2,1,0:T(8,128)} %get-tuple-element.20, pred[4,256,1792]{2,1,0:T(8,128)(4,1)} %copy.27, ...), kind=kOutput, calls=%fused_computation.1 | convolution fusion | flops 1442316288 | bytes 41181184 | tf_op jit(solution)/shard_map/fqhc,fkhc->fhqk/dot_general | solution.py:114
  215.4 6.4 %multiply_bitcast_fusion = f32[4,1792,3,128]{1,3,2,0:T(8,128)S(1)} fusion(bf16[4,3,256,1792]{3,2,1,0:T(8,128)(2,1)} %multiply_convert_fusion, bf16[4,256,3,384]{3,1,0,2:T(8,128)(2,1)} %bitcast.105), kind=kOutput, calls=%fused_computation.12 | convolution fusion | flops 1412038656 | bytes 22806528 | tf_op jit(solution)/shard_map/fhqk,fqhc->fkhc/dot_general | solution.py:124
  221.8 1.1 copy-done.4
  222.9 7.7 %pad_maximum_fusion = f32[4,1792,3,256]{1,3,2,0:T(8,128)} fusion(f32[4,1792,3,128]{1,3,2,0:T(8,128)S(1)} %copy-done.4, f32[4,1792,3,128]{1,3,2,0:T(8,128)S(1)} %multiply_bitcast_fusion), kind=kLoop, calls=%fused_computation | loop fusion | flops 5505024 | bytes 44040192 | tf_op jit(solution)/shard_map/concatenate | solution.py:127
  230.6 21.7 %copy.35 = f32[4,1792,3,256]{3,1,2,0:T(8,128)} copy(f32[4,1792,3,256]{1,3,2,0:T(8,128)} %pad_maximum_fusion) | data formatting | bytes 44040192 | tf_op jit(solution)/shard_map/concatenate | solution.py:127
  252.3 14.5 %slice_bitcast_fusion.6 = (f32[4,256,3,256]{3,1,2,0:T(8,128)S(1)}, f32[4,256,3,256]{3,1,2,0:T(8,128)}, f32[4,256,3,256]{3,1,2,0:T(8,128)}, f32[4,256,3,256]{3,1,...) fusion(f32[4,7,256,3,256]{4,2,1,3,0:T(8,128)} %bitcast.102), kind=kLoop, calls=%fused_computation.51 | loop fusion | bytes 44040192 | tf_op jit(solution)/shard_map/squeeze | solution.py:74
  266.8 11.5 %fusion.91 = (bf16[10,256,3,256]{3,1,2,0:T(8,128)(2,1)}, f32[10,256,3,256]{3,1,2,0:T(8,128)}) fusion(f32[4,256,3,256]{3,1,2,0:T(8,128)} %get-tuple-element.11, f32[4,256,3,256]{3,1,2,0:T(8,128)} %get-tuple-element.12, f32[4,256,3,256]{3,1,2,0:T(8,128)} %get-tuple-element.7, f32[4,256,3,256]{3,1,2,0:T(8,128)} %get-tuple-element.8, ...), kind=kLoop, calls=%fused_computation.126 | loop fusion | flops 13762560 | bytes 33816576 | tf_op jit(solution)/shard_map/convert.2
  278.3 2.9 fusion.92
  281.1 4.4 collective-permute-start.2
  285.5 1.9 collective-permute-start.3
  287.5 10.4 %fusion.79 = bf16[4,256,3,128]{1,3,2,0:T(8,128)(2,1)} fusion(bf16[4,3,256,1792]{3,2,1,0:T(8,128)(2,1)} %multiply_convert_fusion, bf16[4,1792,3,256]{3,1,2,0:T(8,128)(2,1)} %bitcast.111), kind=kOutput, calls=%fused_computation.101 | convolution fusion | flops 1410072576 | bytes 17301504 | tf_op jit(solution)/shard_map/fhqk,fkhc->fqhc/dot_general | solution.py:119
  297.9 2.3 copy.42
  300.2 11.1 %collective-permute-done.2 = bf16[3,256,3,256]{3,1,2,0:T(8,128)(2,1)} collective-permute-done((bf16[3,256,3,256]{3,1,2,0:T(8,128)(2,1)S(1)}, bf16[3,256,3,256]{3,1,2,0:T(8,128)(2,1)}, u32[]{:S(2)}, u32[]{:S(2)}) %collective-permute-start.2) | collective-permute-done | bytes 1179680 | tf_op jit(solution)/shard_map/ppermute | solution.py:22
  311.3 1.6 fusion.82
  312.9 0.0 slice-start.1
  312.9 3.1 fusion.34
  316.1 0.3 pad_maximum_fusion.1
  316.4 0.2 copy.43
  316.7 10.1 %bitcast_convert_fusion = bf16[1024,3072]{1,0:T(8,128)(2,1)} fusion(bf16[1024,3,384]{2,0,1:T(8,128)(2,1)S(1)} %bitcast.113, bf16[3072,3,384]{2,0,1:T(8,128)(2,1)S(1)} %bitcast.119), kind=kOutput, calls=%fused_computation.6 | convolution fusion | flops 7250903040 | bytes 15728640 | tf_op jit(solution)/shard_map/rhc,dhc->rd/dot_general | solution.py:184
  326.8 0.0 reduce-scatter.5.cloned.1.call-update
  326.8 0.0 reduce-scatter.3.cloned.1.call-start
  326.9 1.1 copy-done.7
  328.0 1.2 copy.30
  329.1 6.6 %bitcast_convert_fusion.1 = bf16[1024,3072]{1,0:T(8,128)(2,1)} fusion(bf16[1024,3,128]{2,0,1:T(8,128)(2,1)} %bitcast.114, bf16[3,128,3072]{2,1,0:T(8,128)(2,1)S(1)} %copy-done), kind=kOutput, calls=%fused_computation.7 | convolution fusion | flops 2419064832 | bytes 9437184 | tf_op jit(solution)/shard_map/rhc,hcd->rd/dot_general | solution.py:156
  335.7 0.0 copy-start.13
  335.7 0.0 reduce-scatter.3.cloned.1.call-update
  335.7 89.2 %reduce-scatter.5.cloned.1.call-done = bf16[128,3072]{1,0:T(8,128)(2,1)} async-done(((bf16[1024,3072]{1,0:T(8,128)(2,1)}), bf16[128,3072]{1,0:T(8,128)(2,1)}) %reduce-scatter.5.cloned.1.call-update) | async-done | bytes 786448 | tf_op jit(solution)/shard_map/reduce_scatter | solution.py:183
  424.9 1.6 fusion.69
  426.6 100.5 %reduce-scatter.3.cloned.1.call-done = bf16[128,3072]{1,0:T(8,128)(2,1)} async-done(((bf16[1024,3072]{1,0:T(8,128)(2,1)}), bf16[128,3072]{1,0:T(8,128)(2,1)}) %reduce-scatter.3.cloned.1.call-update) | async-done | bytes 786448 | tf_op jit(solution)/shard_map/reduce_scatter | solution.py:155
  527.2 3.7 fusion.49
  (47 shorter events, 0.1 us)
Async XLA Ops:
  7.2 115.3 %copy-start = (bf16[3,128,3072]{2,1,0:T(8,128)(2,1)S(1)}, bf16[3,128,3072]{2,1,0:T(8,128)(2,1)}, u32[]{:S(2)}) copy-start(bf16[3,128,3072]{2,1,0:T(8,128)(2,1)} %param.13) | copy-start | bytes 7077892
  7.2 6.1 %copy-start.11 = (s32[4,7,4,4]{1,3,2,0:T(4,128)S(1)}, s32[4,7,4,4]{1,3,2,0:T(4,128)}, u32[]{:S(2)}) copy-start(s32[4,7,4,4]{1,3,2,0:T(4,128)} %param.14) | copy-start | bytes 5380
  7.2 97.6 %all-gather.2.cloned.1.call-start = ((), (), s32[]{:S(2)}) async-start(), calls=%async_computation.2 | async-start | bytes 7077888 | tf_op jit(solution)/shard_map/all_gather | solution.py:142
  8.7 1.5 copy-start.14
  10.2 0.5 copy-start.16
  13.2 411.7 %reduce-scatter.5.cloned.1.call-start = ((), (), s32[]{:S(2)}) async-start(), calls=%async_computation.4 | async-start | bytes 7077888 | tf_op jit(solution)/shard_map/reduce_scatter | solution.py:183
  117.3 11.5 %copy-start.2 = (bf16[1024,3,384]{2,0,1:T(8,128)(2,1)}, bf16[1024,3,384]{2,0,1:T(8,128)(2,1)S(1)}, u32[]{:S(2)}) copy-start(bf16[1024,3,384]{2,0,1:T(8,128)(2,1)S(1)} %fusion.35) | copy-start | bytes 7077892
  117.3 5.2 copy-start.12
  119.1 11.7 %copy-start.9 = (pred[4,7,256,4]{2,3,1,0:T(4,128)(4,1)S(1)}, pred[4,7,256,4]{2,3,1,0:T(4,128)(4,1)}, u32[]{:S(2)}) copy-start(pred[4,7,256,4]{2,3,1,0:T(4,128)(4,1)} %eq.23) | copy-start | bytes 86020
  119.1 29.5 %collective-permute-start = (bf16[3,256,3,256]{3,1,0,2:T(8,128)(2,1)}, bf16[3,256,3,256]{3,1,0,2:T(8,128)(2,1)}, u32[]{:S(2)}, u32[]{:S(2)}) collective-permute-start(bf16[3,256,3,256]{3,1,0,2:T(8,128)(2,1)} %get-tuple-element.16), channel_id=1, source_target_pairs={{0,8},{8,16},{16,24},{24,32},{32,40},{40,48},{48,56},{56,64},{64,7... | collective-permute-start | bytes 3538952 | tf_op jit(solution)/shard_map/ppermute | solution.py:22
  128.8 24.4 %collective-permute-start.1 = (bf16[3,256,3,256]{3,1,0,2:T(8,128)(2,1)}, bf16[3,256,3,256]{3,1,0,2:T(8,128)(2,1)S(1)}, u32[]{:S(2)}, u32[]{:S(2)}) collective-permute-start(bf16[3,256,3,256]{3,1,0,2:T(8,128)(2,1)} %get-tuple-element.15), channel_id=1, source_target_pairs={{8,0},{16,8},{24,16},{32,24},{40,32},{48,40},{56,48},{64,56},{72,6... | collective-permute-start | bytes 3538952 | tf_op jit(solution)/shard_map/ppermute | solution.py:24
  151.2 1.8 copy-start.3
  153.5 4.8 copy-start.6
  158.3 13.4 %copy-start.8 = (bf16[1024,3,128]{2,0,1:T(8,128)(2,1)S(1)}, bf16[1024,3,128]{2,0,1:T(8,128)(2,1)}, u32[]{:S(2)}) copy-start(bf16[1024,3,128]{2,0,1:T(8,128)(2,1)} %fusion.74) | copy-start | bytes 2359300
  215.4 7.5 %copy-start.4 = (f32[4,1792,3,128]{1,3,2,0:T(8,128)S(1)}, f32[4,1792,3,128]{1,3,2,0:T(8,128)}, u32[]{:S(2)}) copy-start(f32[4,1792,3,128]{1,3,2,0:T(8,128)} %fusion.22) | copy-start | bytes 33030148
  281.1 30.2 %collective-permute-start.2 = (bf16[3,256,3,256]{3,1,2,0:T(8,128)(2,1)S(1)}, bf16[3,256,3,256]{3,1,2,0:T(8,128)(2,1)}, u32[]{:S(2)}, u32[]{:S(2)}) collective-permute-start(bf16[3,256,3,256]{3,1,2,0:T(8,128)(2,1)S(1)} %get-tuple-element.13), channel_id=1, source_target_pairs={{0,8},{8,16},{16,24},{24,32},{32,40},{40,48},{48,56},{56,64},{64,7... | collective-permute-start | bytes 3538952 | tf_op jit(solution)/shard_map/ppermute | solution.py:22
  285.5 25.8 %collective-permute-start.3 = (bf16[3,256,3,256]{3,1,2,0:T(8,128)(2,1)}, bf16[3,256,3,256]{3,1,2,0:T(8,128)(2,1)}, u32[]{:S(2)}, u32[]{:S(2)}) collective-permute-start(bf16[3,256,3,256]{3,1,2,0:T(8,128)(2,1)} %get-tuple-element.14), channel_id=1, source_target_pairs={{8,0},{16,8},{24,16},{32,24},{40,32},{48,40},{56,48},{64,56},{72,6... | collective-permute-start | bytes 3538952 | tf_op jit(solution)/shard_map/ppermute | solution.py:24
  300.2 12.7 %copy-start.18 = (pred[4]{0:T(512)(128)(4,1)S(1)}, pred[4]{0:T(512)(128)(4,1)}, u32[]{:S(2)}) copy-start(pred[4]{0:T(512)(128)(4,1)} %constant.71.clone.1) | copy-start | bytes 16
  311.3 5.4 slice-start
  312.9 3.2 copy-start.5
  312.9 3.8 slice-start.1
  326.8 1.1 copy-start.7
  326.8 200.3 %reduce-scatter.3.cloned.1.call-start = ((), (), s32[]{:S(2)}) async-start(), calls=%async_computation.3 | async-start | bytes 7077888 | tf_op jit(solution)/shard_map/reduce_scatter | solution.py:155
  335.7 89.3 %copy-start.1 = (bf16[128,3072]{1,0:T(8,128)(2,1)S(1)}, bf16[128,3072]{1,0:T(8,128)(2,1)}, u32[]{:S(2)}) copy-start(bf16[128,3072]{1,0:T(8,128)(2,1)} %param.8) | copy-start | bytes 2359300
  335.7 89.3 %copy-start.10 = (f32[3072]{0:T(1024)S(1)}, f32[3072]{0:T(1024)}, u32[]{:S(2)}) copy-start(f32[3072]{0:T(1024)} %param.9) | copy-start | bytes 36868
  335.7 89.3 %copy-start.15 = (f32[128]{0:T(128)S(1)}, f32[128]{0:T(128)}, u32[]{:S(2)}) copy-start(f32[128]{0:T(128)} %copy-done.14) | copy-start | bytes 1540
  335.7 89.3 %copy-start.17 = (f32[128]{0:T(128)S(1)}, f32[128]{0:T(128)}, u32[]{:S(2)}) copy-start(f32[128]{0:T(128)} %copy-done.16) | copy-start | bytes 1540
  335.7 191.5 %copy-start.13 = (f32[3072]{0:T(1024)S(1)}, f32[3072]{0:T(1024)}, u32[]{:S(2)}) copy-start(f32[3072]{0:T(1024)} %param.11) | copy-start | bytes 36868
Sparse Core Ops, SparseCore 0:
  13.3 91.4 all-gather.1
  327.0 97.9 reduce-scatter.4
  429.4 97.7 reduce-scatter.2
where the time goes:
time: 539 us; the launch traced here: 537 us
  waiting for transfers between devices  295 us (55%)
  matrix products  109 us (20%)
  local copies, waits for them, and re-layouts  63.4 us (12%)
  other arithmetic  43.8 us (8%)
  between operations  14.1 us (3%)
  starting transfers between devices  11.7 us (2%)
    reduce_scatter x1, waiting for transfers between devices, on_device(): lax.psum_scatter(jnp.einsum('rhc,hcd->rd', row_block, out_weight, preferr...  101 us
    all_gather x1, waiting for transfers between devices, on_device(): lax.all_gather(modulated, 'tensor', axis=0, tiled=True)  90.4 us
    reduce_scatter x1, waiting for transfers between devices, on_device(): lax.psum_scatter(jnp.einsum('rhc,dhc->rd', row_block, qkv_weight, preferr...  89.2 us
    concatenate x1, local copies, waits for them, and re-layouts, attend_back(): return (grad_queries, jnp.concatenate([grad_keys, grad_values], axis=-1))  21.7 us
    dot_general x1, matrix products, attend_back(): jnp.einsum('fqhc,fkhc->fhqk', grad_out, value_rows, preferred_element_typ...  17.3 us
    ppermute x2, waiting for transfers between devices, extended(): lax.ppermute(tail, axis, [(i, (i + 1) % count) for i in range(ends)])  14.8 us
    squeeze x1, local copies, waits for them, and re-layouts, spread_windows(): by_offset[:, offset]  14.5 us
    dot_general x1, matrix products, attend(): jnp.einsum('fhqk,fkhc->fqhc', exponent.astype(jnp.bfloat16), value_rows,...  13.6 us
  transfers between devices with their start and end apart: 7, of which 5 were waited for; matrix products, arithmetic and copies ran while one was open for 9% of the time, Pallas kernels for 0%

commit v1 on v0

v1 whole, which is shorter than its diff:
```python
import functools
import math

import jax
import jax.numpy as jnp
from jax import lax
from jax.experimental import pallas as pl
from jax.experimental.pallas import tpu as pltpu
from jax.sharding import PartitionSpec as P

FRAME = 256
TILE = 64
RADIUS = 3
SPAN = 2 * RADIUS + 1
HD = 128
EPSILON = 1e-06
MASKED = -1e30


def norm_rows(inputs, mod_gain, mod_shift):
    floated = inputs.astype(jnp.float32)
    row_mean = jnp.mean(floated, axis=-1, keepdims=True)
    centered = floated - row_mean
    inverse = lax.rsqrt(jnp.mean(centered * centered, axis=-1, keepdims=True) + EPSILON)
    standard = centered * inverse
    return (standard, inverse, (standard * mod_gain + mod_shift).astype(jnp.bfloat16))


def norm_back(grad_norm, standard, inverse, mod_gain, cotangent):
    scaled_grad = grad_norm * mod_gain
    centered = scaled_grad - jnp.mean(scaled_grad, axis=-1, keepdims=True)
    projected = standard * jnp.mean(scaled_grad * standard, axis=-1, keepdims=True)
    return (cotangent.astype(jnp.float32) + inverse * (centered - projected)).astype(jnp.bfloat16)


def mask_bias(tile_mask, first_frame, total_frames):
    frames = lax.broadcasted_iota(jnp.int32, tile_mask.shape, 0) + first_frame
    offsets = lax.broadcasted_iota(jnp.int32, tile_mask.shape, 1)
    query_tile = lax.broadcasted_iota(jnp.int32, tile_mask.shape, 2)
    key_tile = lax.broadcasted_iota(jnp.int32, tile_mask.shape, 3)
    source = frames + offsets - RADIUS
    diagonal = (offsets == RADIUS) & (query_tile == key_tile)
    allowed = ((tile_mask == 1) | diagonal) & (source >= 0) & (source < total_frames)
    bias = jnp.where(allowed, 0.0, MASKED).astype(jnp.float32)
    bias = jnp.transpose(bias, (0, 1, 3, 2))
    return jnp.repeat(bias, TILE, axis=3)


def dot(a, b, dims):
    return lax.dot_general(a, b, (dims, ((), ())), preferred_element_type=jnp.float32)


NN = ((1,), (0,))
NT = ((1,), (1,))


def attention_kernel(
    joined, low, high, grad_out, bias, out, grad_q, own, rims,
    keys, values, keys_t, values_t, exps, grad_k, grad_v,
):
    frame = pl.program_id(1)
    frames = pl.num_programs(1)
    block = 4 * FRAME
    rim = RADIUS * FRAME
    scale = HD ** (-0.5)

    @pl.when(frame == 0)
    def _():
        keys[0:rim, :] = low[0, :, 0:HD]
        keys[rim : rim + block, :] = joined[0, :, HD : 2 * HD]
        keys[rim + block :, :] = high[0, :, 0:HD]
        values[0:rim, :] = low[0, :, HD:]
        values[rim : rim + block, :] = joined[0, :, 2 * HD :]
        values[rim + block :, :] = high[0, :, HD:]
        for part in range(block // FRAME + 2 * RADIUS):
            rows = slice(part * FRAME, (part + 1) * FRAME)
            keys_t[part, :, :] = keys[rows, :].T
            values_t[part, :, :] = values[rows, :].T
        grad_k[...] = jnp.zeros_like(grad_k)
        grad_v[...] = jnp.zeros_like(grad_v)

    own_rows = pl.ds(pl.multiple_of(frame * FRAME, FRAME), FRAME)
    query = joined[0, own_rows, 0:HD]
    grads = grad_out[0, own_rows, :]

    totals = jnp.zeros((8, FRAME), jnp.float32)
    numer = jnp.zeros((HD, FRAME), jnp.float32)
    for offset in range(SPAN):
        rows = pl.ds(pl.multiple_of((frame + offset) * FRAME, FRAME), FRAME)
        scores = dot(keys[rows, :], query, NT) * (scale * math.log2(math.e))
        parts = []
        for tile in range(FRAME // TILE):
            line = bias[0, offset, tile : tile + 1, :]
            parts.append(jnp.exp2(scores[tile * TILE : (tile + 1) * TILE, :] + line))
        exponent = jnp.concatenate(parts, axis=0)
        exps[offset * FRAME : (offset + 1) * FRAME, :] = exponent
        totals += jnp.sum(exponent.reshape(FRAME // 8, 8, FRAME), axis=0)
        numer += dot(values_t[frame + offset], exponent.astype(jnp.bfloat16), NN)
    inverse = 1.0 / jnp.sum(totals, axis=0, keepdims=True)
    output = (numer * inverse).T.astype(jnp.bfloat16)
    out[0] = output
    product = grads.astype(jnp.float32) * output.astype(jnp.float32)
    delta = jnp.sum(product.T, axis=0, keepdims=True)

    grad_query = jnp.zeros((HD, FRAME), jnp.float32)
    for offset in range(SPAN):
        rows = pl.ds(pl.multiple_of((frame + offset) * FRAME, FRAME), FRAME)
        probability = exps[offset * FRAME : (offset + 1) * FRAME, :] * inverse
        grad_probs = dot(values[rows, :], grads, NT)
        grad_v[rows, :] += dot(probability.astype(jnp.bfloat16), grads, NN)
        grad_scores = (probability * (grad_probs - delta)).astype(jnp.bfloat16)
        grad_k[rows, :] += dot(grad_scores, query, NN)
        grad_query += dot(keys_t[frame + offset], grad_scores, NN)
    grad_q[0] = (grad_query * scale).T.astype(jnp.bfloat16)

    @pl.when(frame == frames - 1)
    def _():
        own[0, :, 0:HD] = grad_k[rim : rim + block, :] * scale
        own[0, :, HD:] = grad_v[rim : rim + block, :]
        rims[0, 0:rim, 0:HD] = (grad_k[0:rim, :] * scale).astype(jnp.bfloat16)
        rims[0, rim:, 0:HD] = (grad_k[rim + block :, :] * scale).astype(jnp.bfloat16)
        rims[0, 0:rim, HD:] = grad_v[0:rim, :].astype(jnp.bfloat16)
        rims[0, rim:, HD:] = grad_v[rim + block :, :].astype(jnp.bfloat16)


def attention(joined, low, high, grad_out, bias):
    heads, block, _ = joined.shape
    frames = block // FRAME
    rim = RADIUS * FRAME
    whole = block + 2 * rim
    per_head = lambda head, frame: (head, 0, 0)
    per_frame = lambda head, frame: (head, frame, 0)
    return pl.pallas_call(
        attention_kernel,
        grid=(heads, frames),
        out_shape=(
            jax.ShapeDtypeStruct((heads, block, HD), jnp.bfloat16),
            jax.ShapeDtypeStruct((heads, block, HD), jnp.bfloat16),
            jax.ShapeDtypeStruct((heads, block, 2 * HD), jnp.float32),
            jax.ShapeDtypeStruct((heads, 2 * rim, 2 * HD), jnp.bfloat16),
        ),
        in_specs=[
            pl.BlockSpec((1, block, 3 * HD), per_head),
            pl.BlockSpec((1, rim, 2 * HD), per_head),
            pl.BlockSpec((1, rim, 2 * HD), per_head),
            pl.BlockSpec((1, block, HD), per_head),
            pl.BlockSpec((1, SPAN, 4, FRAME), lambda head, frame: (frame, 0, 0, 0)),
        ],
        out_specs=(
            pl.BlockSpec((1, FRAME, HD), per_frame),
            pl.BlockSpec((1, FRAME, HD), per_frame),
            pl.BlockSpec((1, block, 2 * HD), per_head),
            pl.BlockSpec((1, 2 * rim, 2 * HD), per_head),
        ),
        scratch_shapes=[
            pltpu.VMEM((whole, HD), jnp.bfloat16),
            pltpu.VMEM((whole, HD), jnp.bfloat16),
            pltpu.VMEM((whole // FRAME, HD, FRAME), jnp.bfloat16),
            pltpu.VMEM((whole // FRAME, HD, FRAME), jnp.bfloat16),
            pltpu.VMEM((SPAN * FRAME, FRAME), jnp.float32),
            pltpu.VMEM((whole, HD), jnp.float32),
            pltpu.VMEM((whole, HD), jnp.float32),
        ],
        compiler_params=pltpu.CompilerParams(
            dimension_semantics=("arbitrary", "arbitrary"), vmem_limit_bytes=40 << 20
        ),
        name="attention",
    )(joined, low, high, grad_out, bias)


def on_device(
    activations, mod_gain, mod_shift, out_gate, qkv_weight, out_weight, tile_mask, cotangent
):
    shard_rows = activations.shape[0]
    group_rows = cotangent.shape[0]
    frame_count = tile_mask.shape[0]
    rim = RADIUS * FRAME
    standard, inverse, modulated = norm_rows(activations, mod_gain, mod_shift)
    rows_here = lax.all_gather(modulated, "tensor", tiled=True)
    weight = jnp.transpose(qkv_weight, (1, 0, 2))
    joined = jnp.einsum("rd,hdc->hrc", rows_here, weight, preferred_element_type=jnp.float32)
    joined = joined.astype(jnp.bfloat16)
    count = lax.axis_size("tm")
    upward = [(i, i + 1) for i in range(count - 1)]
    downward = [(i + 1, i) for i in range(count - 1)]
    low = lax.ppermute(joined[:, group_rows - rim :, HD:], "tm", upward)
    high = lax.ppermute(joined[:, :rim, HD:], "tm", downward)
    scaled = (cotangent.astype(jnp.float32) * out_gate).astype(jnp.bfloat16)
    grad_out = jnp.einsum("rd,hcd->hrc", scaled, out_weight, preferred_element_type=jnp.float32)
    grad_out = grad_out.astype(jnp.bfloat16)
    bias = mask_bias(tile_mask, lax.axis_index("tm") * frame_count, frame_count * count)
    output, grad_queries, own, rims = attention(joined, low, high, grad_out, bias)
    projection = lax.psum_scatter(
        jnp.einsum("hrc,hcd->rd", output, out_weight, preferred_element_type=jnp.float32).astype(
            jnp.bfloat16
        ),
        "tensor",
        scatter_dimension=0,
        tiled=True,
    ).astype(jnp.float32)
    layer_out = (activations.astype(jnp.float32) + out_gate * projection).astype(jnp.bfloat16)
    from_above = lax.ppermute(rims[:, :rim], "tm", downward).astype(jnp.float32)
    from_below = lax.ppermute(rims[:, rim:], "tm", upward).astype(jnp.float32)
    spare = group_rows - rim
    grad_pairs = (
        own
        + jnp.pad(from_below, ((0, 0), (0, spare), (0, 0)))
        + jnp.pad(from_above, ((0, 0), (spare, 0), (0, 0)))
    ).astype(jnp.bfloat16)
    grad_joined = jnp.concatenate([grad_queries, grad_pairs], axis=-1)
    grad_norm = lax.psum_scatter(
        jnp.einsum("hrc,hdc->rd", grad_joined, weight, preferred_element_type=jnp.float32).astype(
            jnp.bfloat16
        ),
        "tensor",
        scatter_dimension=0,
        tiled=True,
    ).astype(jnp.float32)
    own_cotangent = lax.dynamic_slice_in_dim(
        cotangent, lax.axis_index("tensor") * shard_rows, shard_rows, 0
    )
    input_grad = norm_back(grad_norm, standard, inverse, mod_gain, own_cotangent)
    return (layer_out, input_grad)


def solution(mesh):
    placed = (
        P(("tm", "tensor"), None),
        P(),
        P(),
        P(),
        P(None, "tensor", None),
        P("tensor", None, None),
        P("tm", None, None, None),
        P("tm", None),
    )
    return jax.shard_map(
        on_device,
        mesh=mesh,
        in_specs=placed,
        out_specs=(P(("tm", "tensor"), None), P(("tm", "tensor"), None)),
        check_vma=False,
    )
```

time: 539 us -> 431 us (0.80)
  matrix products: 109 us -> 33.5 us
  local copies, waits for them, and re-layouts: 63.4 us -> 9.11 us
  other arithmetic: 43.8 us -> 11.7 us
  Pallas kernels: 0 us -> 29.6 us
  waiting for transfers between devices: 295 us -> 320 us
    dot_general x10 -> x4, matrix products: 109 us -> 33.5 us  [the longest x1 12.4 us: on_device(): jnp.einsum('rd,hdc->hrc', rows_here, weight, preferred_element_type=jnp.f...]
    pallas_call x0 -> x1, Pallas kernels: none -> 29.6 us  [attention(): pl.pallas_call(attention_kernel, grid=(heads, frames), out_shape=(jax.Sha...]
    ppermute x4, waiting for transfers between devices: 14.8 us -> 37 us  [the longest x1 23.7 us: on_device(): from_below = lax.ppermute(rims[:, rim:], 'tm', upward).astype(jnp.float32)]
    concatenate x2 -> x0, local copies, waits for them, and re-layouts: 21.9 us -> none  [the longest x1 21.7 us: attend_back(): return (grad_queries, jnp.concatenate([grad_keys, grad_values], axis=-1))]
    squeeze x1 -> x0, local copies, waits for them, and re-layouts: 14.5 us -> none  [spread_windows(): by_offset[:, offset]]
    another operation x2 -> x0, other arithmetic: 11.6 us -> none
    concatenate x2 -> x0, other arithmetic: 8.01 us -> none  [the longest x1 7.68 us: attend_back(): return (grad_queries, jnp.concatenate([grad_keys, grad_values], axis=-1))]
  transfers between devices with their start and end apart: 7 -> 7, of which waited for: 5 -> 5; matrix products, arithmetic and copies ran while one was open for 9% -> 5% of each run, Pallas kernels for 0% -> 0%
where the time goes in v1:
time: 431 us; the launch traced here: 429 us
  waiting for transfers between devices  320 us (74%)
  matrix products  33.5 us (8%)
  Pallas kernels  29.6 us (7%)
  between operations  14 us (3%)
  starting transfers between devices  11.8 us (3%)
  other arithmetic  11.7 us (3%)
  local copies, waits for them, and re-layouts  9.11 us (2%)
    reduce_scatter x1, waiting for transfers between devices, on_device(): lax.psum_scatter(jnp.einsum('hrc,hcd->rd', output, out_weight, preferred_...  100 us
    reduce_scatter x1, waiting for transfers between devices, on_device(): lax.psum_scatter(jnp.einsum('hrc,hdc->rd', grad_joined, weight, preferred...  91.5 us
    all_gather x1, waiting for transfers between devices, on_device(): rows_here = lax.all_gather(modulated, 'tensor', tiled=True)  90.5 us
    pallas_call x1, Pallas kernels, attention(): pl.pallas_call(attention_kernel, grid=(heads, frames), out_shape=(jax.Sha...  29.6 us
    ppermute x1, waiting for transfers between devices, on_device(): from_below = lax.ppermute(rims[:, rim:], 'tm', upward).astype(jnp.float32)  23.7 us
    ppermute x1, waiting for transfers between devices, on_device(): high = lax.ppermute(joined[:, :rim, HD:], 'tm', downward)  13.3 us
    dot_general x1, matrix products, on_device(): jnp.einsum('rd,hdc->hrc', rows_here, weight, preferred_element_type=jnp.f...  12.4 us
    dot_general x1, matrix products, on_device(): jnp.einsum('hrc,hdc->rd', grad_joined, weight, preferred_element_type=jnp...  10.2 us
  transfers between devices with their start and end apart: 7, of which 5 were waited for; matrix products, arithmetic and copies ran while one was open for 5% of the time, Pallas kernels for 0%

profile of v1, /device:TPU:17, one launch (start us, length us, event | category | flops | bytes accessed | tf_op | source)
XLA Modules:
  0.0 429.3 jit_solution(1463724783977594285)
XLA Ops:
  7.2 0.0 copy-start
  7.2 0.0 copy-start.6
  7.2 0.0 copy-start.8
  7.2 0.0 copy-start.10
  7.2 0.0 all-gather.2.cloned.1.call-start
  7.3 1.5 convert_reduce_fusion
  8.7 1.5 fusion.30
  10.2 0.0 copy-done.6
  10.2 0.0 copy-done.8
  10.3 0.0 copy-done.10
  10.3 0.0 copy-start.12
  10.3 1.3 fusion.24
  11.5 0.0 all-gather.2.cloned.1.call-update
  11.6 0.0 reduce-scatter.5.cloned.1.call-start
  11.6 0.5 iota_compare_fusion.1
  12.1 0.5 iota_add_fusion
  12.6 90.5 %all-gather.2.cloned.1.call-done = bf16[1024,3072]{1,0:T(8,128)(2,1)} async-done(((bf16[128,3072]{1,0:T(8,128)(2,1)}), bf16[1024,3072]{1,0:T(8,128)(2,1)}) %all-gather.2.cloned.1.call-update) | async-done | bytes 6291472 | tf_op jit(solution)/shard_map/all_gather | solution.py:179
  103.2 12.4 %convert_bitcast_fusion.joined = bf16[3,1024,384]{2,1,0:T(8,128)(2,1)S(1)} fusion(bf16[3072,3,384]{2,0,1:T(8,128)(2,1)} %param.12, bf16[1024,3072]{1,0:T(8,128)(2,1)} %all-gather.2.cloned.1.call-done), kind=kOutput, calls=%fused_computation.18 | convolution fusion | flops 7248936960 | bytes 15728640 | tf_op jit(solution)/shard_map/rd,hdc->hrc/dot_general | solution.py:181
  115.6 0.0 copy-done.12
  115.6 0.0 copy-start.1
  115.6 0.0 copy-start.9
  115.7 0.0 copy-start.14
  115.7 0.0 copy-start.15
  115.7 1.8 fusion.47
  117.5 0.3 copy-done.1
  117.8 3.0 collective-permute-start.1
  120.8 2.6 collective-permute-start
  123.3 0.0 copy-done.9
  123.4 0.0 copy-done.14
  123.4 0.0 copy-done.15
  123.4 0.7 select_bitcast_fusion
  124.1 1.6 copy.10
  125.6 1.7 broadcast_in_dim.12
  127.3 1.7 reshape.30.bias
  129.1 0.0 copy-done
  129.1 5.7 %fusion.36.grad_out = bf16[3,1024,128]{2,1,0:T(8,128)(2,1)S(1)} fusion(bf16[3,128,3072]{2,1,0:T(8,128)(2,1)S(1)} %copy-done, bf16[1024,3072]{1,0:T(8,128)(2,1)} %param.15, f32[3072]{0:T(1024)} %param.11), kind=kOutput, calls=%fused_computation.36 | convolution fusion | flops 2425749504 | bytes 9449472 | tf_op jit(solution)/shard_map/rd,hcd->hrc/dot_general | solution.py:189
  134.8 13.3 %collective-permute-done.1.high = bf16[3,768,256]{2,1,0:T(8,128)(2,1)S(1)} collective-permute-done((bf16[3,768,256]{2,1,0:T(8,128)(2,1)}, bf16[3,768,256]{2,1,0:T(8,128)(2,1)S(1)}, u32[]{:S(2)}, u32[]{:S(2)}) %collective-permute-start.1) | collective-permute-done | bytes 1179680 | tf_op jit(solution)/shard_map/ppermute | solution.py:187
  148.1 0.0 collective-permute-done.low
  148.1 0.0 copy-done.2
  148.1 0.0 copy-done.3
  148.1 0.0 slice-start
  148.2 29.6 %attention.1 = (bf16[3,1024,128]{2,1,0:T(8,128)(2,1)S(1)}, bf16[3,1024,128]{2,1,0:T(8,128)(2,1)S(1)}, f32[3,1024,256]{2,1,0:T(8,128)S(1)}, bf16[3,1536,256]{2,1,0:T(8,128)(2,1)S(1)}) custom-call(bf16[3,1024,384]{2,1,0:T(8,128)(2,1)S(1)} %copy-done.2, bf16[3,768,256]{2,1,0:T(8,128)(2,1)} %collective-permute-done.low, ...), custom_call_target="tpu_custom_call" | custom-call | tf_op jit(solution)/shard_map/attention/pallas_call | solution.py:133
  177.7 0.0 copy-start.4
  177.7 0.0 slice-start.1
  177.8 0.2 fusion.46
  177.9 0.7 copy-done.4
  178.6 4.0 collective-permute-start.2
  182.7 2.1 collective-permute-start.3
  184.8 23.7 %collective-permute-done.2 = bf16[3,768,256]{2,1,0:T(8,128)(2,1)S(1)} collective-permute-done((bf16[3,768,256]{2,1,0:T(8,128)(2,1)S(1)}, bf16[3,768,256]{2,1,0:T(8,128)(2,1)S(1)}, u32[]{:S(2)}, u32[]{:S(2)}) %collective-permute-start.2) | collective-permute-done | bytes 1179680 | tf_op jit(solution)/shard_map/ppermute | solution.py:203
  208.4 0.0 collective-permute-done.3
  208.4 0.4 add_convert_fusion
  208.9 0.0 slice-done
  208.9 10.2 %bitcast_convert_fusion = bf16[1024,3072]{1,0:T(8,128)(2,1)} fusion(bf16[3072,3,384]{2,0,1:T(8,128)(2,1)S(1)} %bitcast.35, bf16[3,1024,256]{2,1,0:T(8,128)(2,1)S(1)} %add_convert_fusion, bf16[3,1024,128]{2,1,0:T(8,128)(2,1)S(1)} %get-tuple-element.7), kind=kOutput, calls=%fused_computation | convolution fusion | flops 7255621632 | bytes 15728640 | tf_op jit(solution)/shard_map/hrc,hdc->rd/dot_general | solution.py:212
  219.0 0.0 reduce-scatter.5.cloned.1.call-update
  219.1 0.0 reduce-scatter.3.cloned.1.call-start
  219.1 1.1 copy-done.5
  220.2 5.3 %bitcast_convert_fusion.1 = bf16[1024,3072]{1,0:T(8,128)(2,1)} fusion(bf16[3,1024,128]{2,1,0:T(8,128)(2,1)S(1)} %copy-done.5, bf16[3,128,3072]{2,1,0:T(8,128)(2,1)S(1)} %copy-done), kind=kOutput, calls=%fused_computation.1 | convolution fusion | flops 2419064832 | bytes 9437184 | tf_op jit(solution)/shard_map/hrc,hcd->rd/dot_general | solution.py:194
  225.4 0.0 reduce-scatter.3.cloned.1.call-update
  225.5 0.0 copy-start.11
  225.5 91.5 %reduce-scatter.5.cloned.1.call-done = bf16[128,3072]{1,0:T(8,128)(2,1)} async-done(((bf16[1024,3072]{1,0:T(8,128)(2,1)}), bf16[128,3072]{1,0:T(8,128)(2,1)}) %reduce-scatter.5.cloned.1.call-update) | async-done | bytes 786448 | tf_op jit(solution)/shard_map/reduce_scatter | solution.py:211
  317.0 0.0 copy-done.13
  317.0 1.6 fusion.32
  318.7 100.4 %reduce-scatter.3.cloned.1.call-done = bf16[128,3072]{1,0:T(8,128)(2,1)} async-done(((bf16[1024,3072]{1,0:T(8,128)(2,1)}), bf16[128,3072]{1,0:T(8,128)(2,1)}) %reduce-scatter.3.cloned.1.call-update) | async-done | bytes 786448 | tf_op jit(solution)/shard_map/reduce_scatter | solution.py:193
  419.1 3.7 fusion.29
  (12 shorter events, 0.0 us)
Async XLA Ops:
  7.2 121.9 %copy-start = (bf16[3,128,3072]{2,1,0:T(8,128)(2,1)S(1)}, bf16[3,128,3072]{2,1,0:T(8,128)(2,1)}, u32[]{:S(2)}) copy-start(bf16[3,128,3072]{2,1,0:T(8,128)(2,1)} %param.13) | copy-start | bytes 7077892
  7.2 3.1 copy-start.6
  7.2 3.1 copy-start.8
  7.2 3.1 copy-start.10
  7.2 96.0 %all-gather.2.cloned.1.call-start = ((), (), s32[]{:S(2)}) async-start(), calls=%async_computation.2 | async-start | bytes 7077888 | tf_op jit(solution)/shard_map/all_gather | solution.py:179
  10.3 105.4 %copy-start.12 = (f32[128]{0:T(128)}, f32[128]{0:T(128)S(1)}, u32[]{:S(2)}) copy-start(f32[128]{0:T(128)S(1)} %add_rsqrt_fusion) | copy-start | bytes 1540
  11.6 305.4 %reduce-scatter.5.cloned.1.call-start = ((), (), s32[]{:S(2)}) async-start(), calls=%async_computation.4 | async-start | bytes 7077888 | tf_op jit(solution)/shard_map/reduce_scatter | solution.py:211
  115.6 2.1 copy-start.1
  115.6 7.7 %copy-start.9 = (s32[4,7,4,4]{1,3,2,0:T(4,128)S(1)}, s32[4,7,4,4]{1,3,2,0:T(4,128)}, u32[]{:S(2)}) copy-start(s32[4,7,4,4]{1,3,2,0:T(4,128)} %param.14) | copy-start | bytes 5380
  115.7 7.7 %copy-start.14 = (pred[7]{0:T(512)(128)(4,1)S(1)}, pred[7]{0:T(512)(128)(4,1)}, u32[]{:S(2)}) copy-start(pred[7]{0:T(512)(128)(4,1)} %iota_compare_fusion.1) | copy-start | bytes 25
  115.7 7.7 %copy-start.15 = (s32[4]{0:T(128)S(1)}, s32[4]{0:T(128)}, u32[]{:S(2)}) copy-start(s32[4]{0:T(128)} %iota_add_fusion) | copy-start | bytes 52
  117.8 30.4 %collective-permute-start.1 = (bf16[3,768,256]{2,1,0:T(8,128)(2,1)}, bf16[3,768,256]{2,1,0:T(8,128)(2,1)S(1)}, u32[]{:S(2)}, u32[]{:S(2)}) collective-permute-start(bf16[3,768,256]{2,1,0:T(8,128)(2,1)} %get-tuple-element.14), channel_id=1, source_target_pairs={{8,0},{16,8},{24,16},{32,24},{40,32},{48,40},{56,48},{64,56},{72,6... | collective-permute-start | bytes 3538952 | tf_op jit(solution)/shard_map/ppermute | solution.py:187
  120.8 27.4 %collective-permute-start = (bf16[3,768,256]{2,1,0:T(8,128)(2,1)}, bf16[3,768,256]{2,1,0:T(8,128)(2,1)}, u32[]{:S(2)}, u32[]{:S(2)}) collective-permute-start(bf16[3,768,256]{2,1,0:T(8,128)(2,1)} %get-tuple-element.15), channel_id=1, source_target_pairs={{0,8},{8,16},{16,24},{24,32},{32,40},{40,48},{48,56},{56,64},{64,7... | collective-permute-start | bytes 3538952 | tf_op jit(solution)/shard_map/ppermute | solution.py:186
  129.1 19.1 %copy-start.2 = (bf16[3,1024,384]{2,1,0:T(8,128)(2,1)S(1)}, bf16[3,1024,384]{2,1,0:T(8,128)(2,1)}, u32[]{:S(2)}) copy-start(bf16[3,1024,384]{2,1,0:T(8,128)(2,1)} %copy-done.1) | copy-start | bytes 7077892
  129.1 19.1 %copy-start.3 = (f32[4,7,4,256]{3,2,1,0:T(4,128)S(1)}, f32[4,7,4,256]{3,2,1,0:T(4,128)}, u32[]{:S(2)}) copy-start(f32[4,7,4,256]{3,2,1,0:T(4,128)} %reshape.30.bias) | copy-start | bytes 344068
  148.1 60.7 %slice-start = ((s8[7077888]{0:T(1024)(128)(4,1)}), s8[2883584]{0:T(1024)(128)(4,1)S(1)}, s32[]{:S(2)}) async-start(s8[7077888]{0:T(1024)(128)(4,1)} %bitcast.34), calls=%async_computation.5 | async-start | bytes 5767168
  177.7 0.9 copy-start.4
  177.7 31.1 %slice-start.1 = ((s8[7077888]{0:T(1024)(128)(4,1)}), s8[4194304]{0:T(1024)(128)(4,1)S(1)}, s32[]{:S(2)}) async-start(s8[7077888]{0:T(1024)(128)(4,1)} %bitcast.34), calls=%async_computation.6 | async-start | bytes 8388608
  178.6 29.8 %collective-permute-start.2 = (bf16[3,768,256]{2,1,0:T(8,128)(2,1)S(1)}, bf16[3,768,256]{2,1,0:T(8,128)(2,1)S(1)}, u32[]{:S(2)}, u32[]{:S(2)}) collective-permute-start(bf16[3,768,256]{2,1,0:T(8,128)(2,1)S(1)} %get-tuple-element.12), channel_id=1, source_target_pairs={{0,8},{8,16},{16,24},{24,32},{32,40},{40,48},{48,56},{56,64},{64,7... | collective-permute-start | bytes 3538952 | tf_op jit(solution)/shard_map/ppermute | solution.py:203
  182.7 25.8 %collective-permute-start.3 = (bf16[3,768,256]{2,1,0:T(8,128)(2,1)S(1)}, bf16[3,768,256]{2,1,0:T(8,128)(2,1)S(1)}, u32[]{:S(2)}, u32[]{:S(2)}) collective-permute-start(bf16[3,768,256]{2,1,0:T(8,128)(2,1)S(1)} %get-tuple-element.13), channel_id=1, source_target_pairs={{8,0},{16,8},{24,16},{32,24},{40,32},{48,40},{56,48},{64,56},{72,6... | collective-permute-start | bytes 3538952 | tf_op jit(solution)/shard_map/ppermute | solution.py:202
  219.0 1.1 copy-start.5
  219.1 200.0 %reduce-scatter.3.cloned.1.call-start = ((), (), s32[]{:S(2)}) async-start(), calls=%async_computation.3 | async-start | bytes 7077888 | tf_op jit(solution)/shard_map/reduce_scatter | solution.py:193
  225.4 91.6 %copy-start.7 = (bf16[128,3072]{1,0:T(8,128)(2,1)S(1)}, bf16[128,3072]{1,0:T(8,128)(2,1)}, u32[]{:S(2)}) copy-start(bf16[128,3072]{1,0:T(8,128)(2,1)} %param.8) | copy-start | bytes 2359300
  225.4 91.6 %copy-start.13 = (f32[128]{0:T(128)S(1)}, f32[128]{0:T(128)}, u32[]{:S(2)}) copy-start(f32[128]{0:T(128)} %copy-done.12) | copy-start | bytes 1540
  225.5 193.6 %copy-start.11 = (f32[3072]{0:T(1024)S(1)}, f32[3072]{0:T(1024)}, u32[]{:S(2)}) copy-start(f32[3072]{0:T(1024)} %param.11) | copy-start | bytes 36868
Sparse Core Ops, SparseCore 0:
  11.7 91.4 all-gather.1
  219.2 97.7 reduce-scatter.4
  321.4 97.6 reduce-scatter.2

commit v2 on v1

--- a/solution.py
+++ b/solution.py
@@ -168,6 +168,246 @@
     )(joined, low, high, grad_out, bias)
 
 
+SIXTH = 512
+LOW = (0, 3)
+HIGH = (3, 6)
+
+
+def cols(span):
+    return slice(span[0] * SIXTH, span[1] * SIXTH)
+
+
+def ring_places():
+    me = lax.axis_index("tensor")
+    z, x = me // 4, me % 4
+
+    def place(other, shift):
+        return ((z + other) % 2) * 4 + (x + shift) % 4
+
+    return place
+
+
+def meet(neighbours):
+    barrier = pltpu.get_barrier_semaphore()
+    for neighbour in neighbours:
+        pl.semaphore_signal(
+            barrier, inc=1, device_id={"tensor": neighbour}, device_id_type=pl.DeviceIdType.MESH
+        )
+    pl.semaphore_wait(barrier, len(neighbours))
+
+
+def gather_kernel(block, out, send, recv, own_sem):
+    place = ring_places()
+    up, down, across = place(0, 1), place(0, -1), place(1, 0)
+    size = block.shape[0]
+
+    def rows(other, shift):
+        return pl.ds(pl.multiple_of(place(other, shift) * size, size), size)
+
+    meet((up, down, across))
+    started = []
+
+    def push(number, target, source, other, shift, span):
+        where = out.at[rows(other, shift), cols(span)]
+        if source is None:
+            source = where
+        else:
+            source = source.at[:, cols(span)]
+        copy = pltpu.make_async_remote_copy(
+            src_ref=source,
+            dst_ref=where,
+            send_sem=send.at[number],
+            recv_sem=recv.at[number],
+            device_id={"tensor": target},
+            device_id_type=pl.DeviceIdType.MESH,
+        )
+        copy.start()
+        started.append(copy)
+
+    def arrived(number, other, shift, span):
+        where = out.at[rows(other, shift), cols(span)]
+        pltpu.make_async_remote_copy(
+            src_ref=where,
+            dst_ref=where,
+            send_sem=send.at[number],
+            recv_sem=recv.at[number],
+            device_id={"tensor": up},
+            device_id_type=pl.DeviceIdType.MESH,
+        ).wait_recv()
+
+    push(0, up, block, 0, 0, LOW)
+    push(5, down, block, 0, 0, HIGH)
+    push(10, across, block, 0, 0, HIGH)
+    push(1, up, block, 0, 0, HIGH)
+    push(6, down, block, 0, 0, LOW)
+    push(11, across, block, 0, 0, LOW)
+    own = pltpu.make_async_copy(block, out.at[rows(0, 0), :], own_sem)
+    own.start()
+    arrived(0, 0, -1, LOW)
+    push(2, up, None, 0, -1, LOW)
+    push(12, across, None, 0, -1, LOW)
+    arrived(5, 0, 1, HIGH)
+    push(7, down, None, 0, 1, HIGH)
+    arrived(10, 1, 0, HIGH)
+    push(3, up, None, 1, 0, HIGH)
+    push(8, down, None, 1, 0, HIGH)
+    arrived(6, 0, 1, LOW)
+    push(13, across, None, 0, 1, LOW)
+    arrived(12, 1, -1, LOW)
+    push(4, up, None, 1, -1, (0, 2))
+    arrived(7, 0, 2, HIGH)
+    push(14, across, None, 0, 2, (4, 6))
+    arrived(13, 1, 1, LOW)
+    arrived(8, 1, 1, HIGH)
+    push(9, down, None, 1, 1, (2, 4))
+    arrived(1, 0, -1, HIGH)
+    arrived(11, 1, 0, LOW)
+    arrived(2, 0, 2, LOW)
+    arrived(3, 1, -1, HIGH)
+    arrived(4, 1, 2, (0, 2))
+    arrived(9, 1, 2, (2, 4))
+    arrived(14, 1, 2, (4, 6))
+    for copy in started:
+        copy.wait_send()
+    own.wait()
+
+
+def gather_rows(block):
+    size, width = block.shape
+    return pl.pallas_call(
+        gather_kernel,
+        out_shape=jax.ShapeDtypeStruct((8 * size, width), block.dtype),
+        in_specs=[pl.BlockSpec(memory_space=pltpu.VMEM)],
+        out_specs=pl.BlockSpec(memory_space=pltpu.VMEM),
+        scratch_shapes=[
+            pltpu.SemaphoreType.DMA((15,)),
+            pltpu.SemaphoreType.DMA((15,)),
+            pltpu.SemaphoreType.DMA(()),
+        ],
+        compiler_params=pltpu.CompilerParams(
+            collective_id=0, has_side_effects=True, vmem_limit_bytes=40 << 20
+        ),
+        cost_estimate=pl.CostEstimate(
+            flops=0, bytes_accessed=180 << 20, transcendentals=0
+        ),
+        name="gather_rows",
+    )(block)
+
+
+def scatter_kernel(partial, out, landing, staged, send, recv):
+    place = ring_places()
+    up, down, across = place(0, 1), place(0, -1), place(1, 0)
+    size = out.shape[0]
+
+    def rows(other, shift):
+        return pl.ds(pl.multiple_of(place(other, shift) * size, size), size)
+
+    meet((up, down, across))
+    started = []
+
+    def push(number, target, source, width):
+        copy = pltpu.make_async_remote_copy(
+            src_ref=source,
+            dst_ref=landing.at[number, :, 0 : width * SIXTH],
+            send_sem=send.at[number],
+            recv_sem=recv.at[number],
+            device_id={"tensor": target},
+            device_id_type=pl.DeviceIdType.MESH,
+        )
+        copy.start()
+        started.append(copy)
+
+    def plain(number, target, other, shift, span):
+        push(number, target, partial.at[rows(other, shift), cols(span)], span[1] - span[0])
+
+    def arrived(number, width=3):
+        where = landing.at[number, :, 0 : width * SIXTH]
+        pltpu.make_async_remote_copy(
+            src_ref=where,
+            dst_ref=where,
+            send_sem=send.at[number],
+            recv_sem=recv.at[number],
+            device_id={"tensor": up},
+            device_id_type=pl.DeviceIdType.MESH,
+        ).wait_recv()
+
+    def summed(number, target, slot, other, shift, span, parts):
+        for piece in range(span[0], span[1]):
+            total = partial[rows(other, shift), cols((piece, piece + 1))].astype(jnp.float32)
+            for landed, first, over in parts:
+                if over[0] <= piece < over[1]:
+                    total += landing[landed, :, cols((piece - first, piece - first + 1))].astype(jnp.float32)
+            staged[slot, :, cols((piece - span[0], piece - span[0] + 1))] = total.astype(jnp.bfloat16)
+        push(number, target, staged.at[slot], 3)
+
+    plain(0, down, 1, 2, (0, 2))
+    plain(5, up, 1, 2, (2, 4))
+    plain(10, across, 1, 2, (4, 6))
+    plain(1, down, 1, -1, HIGH)
+    plain(2, down, 0, 2, LOW)
+    plain(3, down, 0, -1, HIGH)
+    arrived(5, 2)
+    summed(6, up, 0, 1, 1, HIGH, ((5, 2, (2, 4)),))
+    arrived(0, 2)
+    summed(11, across, 1, 1, -1, LOW, ((0, 0, (0, 2)),))
+    arrived(10, 2)
+    summed(7, up, 2, 0, 2, HIGH, ((10, 4, (4, 6)),))
+    summed(12, across, 3, 1, 1, LOW, ((5, 2, (2, 4)),))
+    plain(13, across, 1, 0, LOW)
+    arrived(2)
+    arrived(11)
+    summed(4, down, 4, 0, -1, LOW, ((2, 0, LOW), (11, 0, LOW)))
+    arrived(12)
+    summed(8, up, 5, 0, 1, LOW, ((12, 0, LOW),))
+    arrived(7)
+    summed(9, up, 6, 0, 1, HIGH, ((7, 3, HIGH),))
+    arrived(1)
+    arrived(6)
+    summed(14, across, 7, 1, 0, HIGH, ((1, 3, HIGH), (6, 3, HIGH)))
+    arrived(4)
+    arrived(8)
+    arrived(13)
+    for piece in range(3):
+        total = partial[rows(0, 0), cols((piece, piece + 1))].astype(jnp.float32)
+        for landed in (4, 8, 13):
+            total += landing[landed, :, cols((piece, piece + 1))].astype(jnp.float32)
+        out[:, cols((piece, piece + 1))] = total
+    arrived(3)
+    arrived(9)
+    arrived(14)
+    for piece in range(3):
+        total = partial[rows(0, 0), cols((piece + 3, piece + 4))].astype(jnp.float32)
+        for landed in (3, 9, 14):
+            total += landing[landed, :, cols((piece, piece + 1))].astype(jnp.float32)
+        out[:, cols((piece + 3, piece + 4))] = total
+    for copy in started:
+        copy.wait_send()
+
+
+def scatter_rows(partial, collective_id, name):
+    height, width = partial.shape
+    size = height // 8
+    return pl.pallas_call(
+        scatter_kernel,
+        out_shape=jax.ShapeDtypeStruct((size, width), jnp.float32),
+        in_specs=[pl.BlockSpec(memory_space=pltpu.VMEM)],
+        out_specs=pl.BlockSpec(memory_space=pltpu.VMEM),
+        scratch_shapes=[
+            pltpu.VMEM((15, size, width // 2), jnp.bfloat16),
+            pltpu.VMEM((8, size, width // 2), jnp.bfloat16),
+            pltpu.SemaphoreType.DMA((15,)),
+            pltpu.SemaphoreType.DMA((15,)),
+        ],
+        compiler_params=pltpu.CompilerParams(
+            collective_id=collective_id, has_side_effects=True, vmem_limit_bytes=40 << 20
+        ),
+        cost_estimate=pl.CostEstimate(
+            flops=0, bytes_accessed=180 << 20, transcendentals=0
+        ),
+        name=name,
+    )(partial)
+
+
 def on_device(
     activations, mod_gain, mod_shift, out_gate, qkv_weight, out_weight, tile_mask, cotangent
 ):
@@ -176,7 +416,7 @@
     frame_count = tile_mask.shape[0]
     rim = RADIUS * FRAME
     standard, inverse, modulated = norm_rows(activations, mod_gain, mod_shift)
-    rows_here = lax.all_gather(modulated, "tensor", tiled=True)
+    rows_here = gather_rows(modulated)
     weight = jnp.transpose(qkv_weight, (1, 0, 2))
     joined = jnp.einsum("rd,hdc->hrc", rows_here, weight, preferred_element_type=jnp.float32)
     joined = joined.astype(jnp.bfloat16)
@@ -190,14 +430,8 @@
     grad_out = grad_out.astype(jnp.bfloat16)
     bias = mask_bias(tile_mask, lax.axis_index("tm") * frame_count, frame_count * count)
     output, grad_queries, own, rims = attention(joined, low, high, grad_out, bias)
-    projection = lax.psum_scatter(
-        jnp.einsum("hrc,hcd->rd", output, out_weight, preferred_element_type=jnp.float32).astype(
-            jnp.bfloat16
-        ),
-        "tensor",
-        scatter_dimension=0,
-        tiled=True,
-    ).astype(jnp.float32)
+    projected = jnp.einsum("hrc,hcd->rd", output, out_weight, preferred_element_type=jnp.float32)
+    projection = scatter_rows(projected.astype(jnp.bfloat16), 1, "scatter_out")
     layer_out = (activations.astype(jnp.float32) + out_gate * projection).astype(jnp.bfloat16)
     from_above = lax.ppermute(rims[:, :rim], "tm", downward).astype(jnp.float32)
     from_below = lax.ppermute(rims[:, rim:], "tm", upward).astype(jnp.float32)
@@ -208,14 +442,8 @@
         + jnp.pad(from_above, ((0, 0), (spare, 0), (0, 0)))
     ).astype(jnp.bfloat16)
     grad_joined = jnp.concatenate([grad_queries, grad_pairs], axis=-1)
-    grad_norm = lax.psum_scatter(
-        jnp.einsum("hrc,hdc->rd", grad_joined, weight, preferred_element_type=jnp.float32).astype(
-            jnp.bfloat16
-        ),
-        "tensor",
-        scatter_dimension=0,
-        tiled=True,
-    ).astype(jnp.float32)
+    grad_rows = jnp.einsum("hrc,hdc->rd", grad_joined, weight, preferred_element_type=jnp.float32)
+    grad_norm = scatter_rows(grad_rows.astype(jnp.bfloat16), 2, "scatter_grad")
     own_cotangent = lax.dynamic_slice_in_dim(
         cotangent, lax.axis_index("tensor") * shard_rows, shard_rows, 0
     )

time: 431 us -> 255 us (0.59)
  waiting for transfers between devices: 320 us -> 12.1 us
  Pallas kernels: 29.6 us -> 177 us
  between operations: 14 us -> 0.96 us
    reduce_scatter x2 -> x0, waiting for transfers between devices: 192 us -> none  [the longest x1 100 us: on_device(): lax.psum_scatter(jnp.einsum('hrc,hcd->rd', output, out_weight, preferred_...]
    pallas_call x0 -> x3, Pallas kernels: none -> 147 us  [the longest x2 101 us: scatter_rows(): pl.pallas_call(scatter_kernel, out_shape=jax.ShapeDtypeStruct((size, widt...]
    all_gather x1 -> x0, waiting for transfers between devices: 90.5 us -> none  [on_device(): rows_here = lax.all_gather(modulated, 'tensor', tiled=True)]
    ppermute x1, waiting for transfers between devices: 23.7 us -> 0.01 us  [on_device(): from_below = lax.ppermute(rims[:, rim:], 'tm', upward).astype(jnp.float32)]
  transfers between devices with their start and end apart: 7 -> 4, of which waited for: 5 -> 1; matrix products, arithmetic and copies ran while one was open for 5% -> 7% of each run, Pallas kernels for 0% -> 25%
where the time goes in v2:
time: 255 us; the launch traced here: 253 us
  Pallas kernels  177 us (69%)
  matrix products  29.5 us (12%)
  starting transfers between devices  12.2 us (5%)
  waiting for transfers between devices  12.1 us (5%)
  other arithmetic  10.9 us (4%)
  local copies, waits for them, and re-layouts  10.3 us (4%)
    pallas_call x2, Pallas kernels, scatter_rows(): pl.pallas_call(scatter_kernel, out_shape=jax.ShapeDtypeStruct((size, widt...  101 us
    pallas_call x1, Pallas kernels, gather_rows(): pl.pallas_call(gather_kernel, out_shape=jax.ShapeDtypeStruct((8 * size, w...  45.9 us
    pallas_call x1, Pallas kernels, attention(): pl.pallas_call(attention_kernel, grid=(heads, frames), out_shape=(jax.Sha...  29.7 us
    ppermute x1, waiting for transfers between devices, on_device(): high = lax.ppermute(joined[:, :rim, HD:], 'tm', downward)  12.1 us
    dot_general x1, matrix products, on_device(): jnp.einsum('hrc,hdc->rd', grad_joined, weight, preferred_element_type=jnp...  10.6 us
    dot_general x1, matrix products, on_device(): jnp.einsum('rd,hdc->hrc', rows_here, weight, preferred_element_type=jnp.f...  8.51 us
    dot_general x1, matrix products, on_device(): jnp.einsum('rd,hcd->hrc', scaled, out_weight, preferred_element_type=jnp....  5.69 us
  transfers between devices with their start and end apart: 4, of which 1 were waited for; matrix products, arithmetic and copies ran while one was open for 7% of the time, Pallas kernels for 25%

profile of v2, /device:TPU:17, one launch (start us, length us, event | category | flops | bytes accessed | tf_op | source)
XLA Modules:
  0.0 253.0 jit_solution(1406512301534030878)
XLA Ops:
  0.6 0.0 copy-start
  0.6 0.0 copy-start.9
  0.7 0.0 copy-start.11
  0.7 0.0 copy-start.12
  0.7 1.5 convert_reduce_fusion
  2.2 1.5 fusion.30
  3.7 0.0 copy-done.9
  3.7 0.0 copy-done.11
  3.7 0.0 copy-done.12
  3.7 0.0 copy-start.14
  3.7 0.4 fusion.24.block
  4.1 0.0 copy-start.16
  4.1 45.9 %gather_rows.1 = bf16[1024,3072]{1,0:T(8,128)(2,1)S(1)} custom-call(bf16[128,3072]{1,0:T(8,128)(2,1)S(1)} %fusion.24.block), custom_call_target="tpu_custom_call" | custom-call | bytes 188743680 | tf_op jit(solution)/shard_map/gather_rows/pallas_call | solution.py:277
  50.0 0.0 copy-done.14
  50.0 0.0 copy-done.16
  50.0 8.5 %convert_bitcast_fusion.joined = bf16[3,1024,384]{2,1,0:T(8,128)(2,1)S(1)} fusion(bf16[3072,3,384]{2,0,1:T(8,128)(2,1)S(1)} %copy-done.16, bf16[1024,3072]{1,0:T(8,128)(2,1)S(1)} %gather_rows.1), kind=kOutput, calls=%fused_computation.18 | convolution fusion | flops 7248936960 | bytes 15728640 | tf_op jit(solution)/shard_map/rd,hdc->hrc/dot_general | solution.py:421
  58.6 0.0 copy-start.1
  58.6 1.8 fusion.46
  60.3 0.4 copy-done.1
  60.7 3.5 %collective-permute-start.1 = (bf16[3,768,256]{2,1,0:T(8,128)(2,1)}, bf16[3,768,256]{2,1,0:T(8,128)(2,1)S(1)}, u32[]{:S(2)}, u32[]{:S(2)}) collective-permute-start(bf16[3,768,256]{2,1,0:T(8,128)(2,1)} %get-tuple-element.14), channel_id=1, source_target_pairs={{8,0},{16,8},{24,16},{32,24},{40,32},{48,40},{56,48},{64,56},{72,6... | collective-permute-start | bytes 3538952 | tf_op jit(solution)/shard_map/ppermute | solution.py:427
  64.3 2.5 %collective-permute-start = (bf16[3,768,256]{2,1,0:T(8,128)(2,1)}, bf16[3,768,256]{2,1,0:T(8,128)(2,1)}, u32[]{:S(2)}, u32[]{:S(2)}) collective-permute-start(bf16[3,768,256]{2,1,0:T(8,128)(2,1)} %get-tuple-element.15), channel_id=1, source_target_pairs={{0,8},{8,16},{16,24},{24,32},{32,40},{40,48},{48,56},{56,64},{64,7... | collective-permute-start | bytes 3538952 | tf_op jit(solution)/shard_map/ppermute | solution.py:426
  66.8 0.5 iota_compare_fusion.1
  67.3 1.5 select_bitcast_fusion
  68.8 1.6 copy.10
  70.4 1.7 broadcast_in_dim.12
  72.1 1.7 reshape.30.bias
  73.8 0.0 copy-done
  73.8 0.0 copy-start.2
  73.8 0.0 copy-start.5
  73.8 5.7 %fusion.35.grad_out = bf16[3,1024,128]{2,1,0:T(8,128)(2,1)S(1)} fusion(bf16[3,128,3072]{2,1,0:T(8,128)(2,1)S(1)} %copy-done, bf16[1024,3072]{1,0:T(8,128)(2,1)} %param.15, f32[3072]{0:T(1024)} %param.11), kind=kOutput, calls=%fused_computation.35 | convolution fusion | flops 2425749504 | bytes 9449472 | tf_op jit(solution)/shard_map/rd,hcd->hrc/dot_general | solution.py:429
  79.5 12.1 %collective-permute-done.1.high = bf16[3,768,256]{2,1,0:T(8,128)(2,1)S(1)} collective-permute-done((bf16[3,768,256]{2,1,0:T(8,128)(2,1)}, bf16[3,768,256]{2,1,0:T(8,128)(2,1)S(1)}, u32[]{:S(2)}, u32[]{:S(2)}) %collective-permute-start.1) | collective-permute-done | bytes 1179680 | tf_op jit(solution)/shard_map/ppermute | solution.py:427
  91.6 0.0 collective-permute-done.low
  91.6 0.0 copy-done.2
  91.6 0.0 copy-done.5
  91.6 29.7 %attention.1 = (bf16[3,1024,128]{2,1,0:T(8,128)(2,1)S(1)}, bf16[3,1024,128]{2,1,0:T(8,128)(2,1)S(1)}, f32[3,1024,256]{2,1,0:T(8,128)S(1)}, bf16[3,1536,256]{2,1,0:T(8,128)(2,1)S(1)}) custom-call(bf16[3,1024,384]{2,1,0:T(8,128)(2,1)S(1)} %copy-done.2, bf16[3,768,256]{2,1,0:T(8,128)(2,1)} %collective-permute-done.low, ...), custom_call_target="tpu_custom_call" | custom-call | tf_op jit(solution)/shard_map/attention/pallas_call | solution.py:133
  121.4 0.0 copy-start.3
  121.4 0.0 copy-start.6
  121.4 0.0 copy-start.8
  121.4 1.7 fusion.45
  123.1 0.6 copy-done.3
  123.7 0.3 copy-done.6
  124.0 0.3 copy-done.8
  124.2 4.0 %collective-permute-start.2 = (bf16[3,768,256]{2,1,0:T(8,128)(2,1)}, bf16[3,768,256]{2,1,0:T(8,128)(2,1)S(1)}, u32[]{:S(2)}, u32[]{:S(2)}) collective-permute-start(bf16[3,768,256]{2,1,0:T(8,128)(2,1)} %get-tuple-element.12), channel_id=1, source_target_pairs={{0,8},{8,16},{16,24},{24,32},{32,40},{40,48},{48,56},{56,64},{64,7... | collective-permute-start | bytes 3538952 | tf_op jit(solution)/shard_map/ppermute | solution.py:437
  128.3 2.1 collective-permute-start.3
  130.4 4.8 %bitcast_convert_fusion.1.partial = bf16[1024,3072]{1,0:T(8,128)(2,1)S(1)} fusion(bf16[3,1024,128]{2,1,0:T(8,128)(2,1)} %copy-done.8, bf16[3,128,3072]{2,1,0:T(8,128)(2,1)S(1)} %copy-done), kind=kOutput, calls=%fused_computation.1 | convolution fusion | flops 2419064832 | bytes 9437184 | tf_op jit(solution)/shard_map/hrc,hcd->rd/dot_general | solution.py:433
  135.2 0.0 copy-start.4
  135.2 63.6 %scatter_out.1 = f32[128,3072]{1,0:T(8,128)S(1)} custom-call(bf16[1024,3072]{1,0:T(8,128)(2,1)S(1)} %bitcast_convert_fusion.1.partial), custom_call_target="tpu_custom_call" | custom-call | bytes 188743680 | tf_op jit(solution)/shard_map/scatter_out/pallas_call | solution.py:390
  198.7 0.0 collective-permute-done.2
  198.8 0.0 collective-permute-done.3
  198.8 0.0 copy-done.4
  198.8 0.0 copy-start.7
  198.8 1.9 add_convert_fusion
  200.7 0.0 copy-done.7
  200.7 10.6 %bitcast_convert_fusion.partial = bf16[1024,3072]{1,0:T(8,128)(2,1)S(1)} fusion(bf16[3072,3,384]{2,0,1:T(8,128)(2,1)} %param.12, bf16[3,1024,256]{2,1,0:T(8,128)(2,1)S(1)} %add_convert_fusion, bf16[3,1024,128]{2,1,0:T(8,128)(2,1)S(1)} %copy-done.7), kind=kOutput, calls=%fused_computation | convolution fusion | flops 7255621632 | bytes 15728640 | tf_op jit(solution)/shard_map/hrc,hdc->rd/dot_general | solution.py:445
  211.2 0.0 copy-start.10
  211.2 0.0 copy-start.15
  211.3 37.8 %scatter_grad.1 = f32[128,3072]{1,0:T(8,128)S(1)} custom-call(bf16[1024,3072]{1,0:T(8,128)(2,1)S(1)} %bitcast_convert_fusion.partial), custom_call_target="tpu_custom_call" | custom-call | bytes 188743680 | tf_op jit(solution)/shard_map/scatter_grad/pallas_call | solution.py:390
  249.0 0.0 copy-done.10
  249.1 0.0 copy-done.15
  249.1 0.0 copy-start.13
  249.1 0.5 multiply_reduce_fusion
  249.6 0.2 copy-done.13
  249.8 3.2 %fusion.29 = (bf16[128,3072]{1,0:T(8,128)(2,1)}, bf16[128,3072]{1,0:T(8,128)(2,1)}) fusion(bf16[128,3072]{1,0:T(8,128)(2,1)S(1)} %copy-done.10, f32[128,3072]{1,0:T(8,128)S(1)} %scatter_grad.1, f32[128]{0:T(128)S(1)} %get-tuple-element.18, f32[128]{0:T(128)S(1)} %get-tuple-element.19, bf16[1024,3072]{1,0:T(8,128)(2,1)} %param.15, s32[]{:T(128)S(6)} %select_n.8, ...), kind=kLoop, calls=%fused_computation.30 | loop fusion | flops 5505024 | bytes 6318084 | tf_op jit(solution)/shard_map/convert_element_type | solution.py:33
  (4 shorter events, 0.0 us)
Async XLA Ops:
  0.6 73.2 %copy-start = (bf16[3,128,3072]{2,1,0:T(8,128)(2,1)S(1)}, bf16[3,128,3072]{2,1,0:T(8,128)(2,1)}, u32[]{:S(2)}) copy-start(bf16[3,128,3072]{2,1,0:T(8,128)(2,1)} %param.13) | copy-start | bytes 7077892
  0.6 3.0 %copy-start.9 = (bf16[128,3072]{1,0:T(8,128)(2,1)S(1)}, bf16[128,3072]{1,0:T(8,128)(2,1)}, u32[]{:S(2)}) copy-start(bf16[128,3072]{1,0:T(8,128)(2,1)} %param.8) | copy-start | bytes 2359300
  0.7 3.0 %copy-start.11 = (f32[3072]{0:T(1024)S(1)}, f32[3072]{0:T(1024)}, u32[]{:S(2)}) copy-start(f32[3072]{0:T(1024)} %param.9) | copy-start | bytes 36868
  0.7 3.0 %copy-start.12 = (f32[3072]{0:T(1024)S(1)}, f32[3072]{0:T(1024)}, u32[]{:S(2)}) copy-start(f32[3072]{0:T(1024)} %param.10) | copy-start | bytes 36868
  3.7 46.3 %copy-start.14 = (f32[128]{0:T(128)}, f32[128]{0:T(128)S(1)}, u32[]{:S(2)}) copy-start(f32[128]{0:T(128)S(1)} %add_rsqrt_fusion) | copy-start | bytes 1540
  4.1 45.9 %copy-start.16 = (bf16[3072,3,384]{2,0,1:T(8,128)(2,1)S(1)}, bf16[3072,3,384]{2,0,1:T(8,128)(2,1)}, u32[]{:S(2)}) copy-start(bf16[3072,3,384]{2,0,1:T(8,128)(2,1)} %param.12) | copy-start | bytes 21233668
  58.6 2.2 copy-start.1
  60.7 30.9 %collective-permute-start.1 = (bf16[3,768,256]{2,1,0:T(8,128)(2,1)}, bf16[3,768,256]{2,1,0:T(8,128)(2,1)S(1)}, u32[]{:S(2)}, u32[]{:S(2)}) collective-permute-start(bf16[3,768,256]{2,1,0:T(8,128)(2,1)} %get-tuple-element.14), channel_id=1, source_target_pairs={{8,0},{16,8},{24,16},{32,24},{40,32},{48,40},{56,48},{64,56},{72,6... | collective-permute-start | bytes 3538952 | tf_op jit(solution)/shard_map/ppermute | solution.py:427
  64.3 27.4 %collective-permute-start = (bf16[3,768,256]{2,1,0:T(8,128)(2,1)}, bf16[3,768,256]{2,1,0:T(8,128)(2,1)}, u32[]{:S(2)}, u32[]{:S(2)}) collective-permute-start(bf16[3,768,256]{2,1,0:T(8,128)(2,1)} %get-tuple-element.15), channel_id=1, source_target_pairs={{0,8},{8,16},{16,24},{24,32},{32,40},{40,48},{48,56},{56,64},{64,7... | collective-permute-start | bytes 3538952 | tf_op jit(solution)/shard_map/ppermute | solution.py:426
  73.8 17.8 %copy-start.2 = (bf16[3,1024,384]{2,1,0:T(8,128)(2,1)S(1)}, bf16[3,1024,384]{2,1,0:T(8,128)(2,1)}, u32[]{:S(2)}) copy-start(bf16[3,1024,384]{2,1,0:T(8,128)(2,1)} %copy-done.1) | copy-start | bytes 7077892
  73.8 17.8 %copy-start.5 = (f32[4,7,4,256]{3,2,1,0:T(4,128)S(1)}, f32[4,7,4,256]{3,2,1,0:T(4,128)}, u32[]{:S(2)}) copy-start(f32[4,7,4,256]{3,2,1,0:T(4,128)} %reshape.30.bias) | copy-start | bytes 344068
  121.4 2.4 copy-start.3
  121.4 2.6 %copy-start.6 = (bf16[3,1024,128]{2,1,0:T(8,128)(2,1)}, bf16[3,1024,128]{2,1,0:T(8,128)(2,1)S(1)}, u32[]{:S(2)}) copy-start(bf16[3,1024,128]{2,1,0:T(8,128)(2,1)S(1)} %get-tuple-element.7) | copy-start | bytes 2359300
  121.4 2.9 %copy-start.8 = (bf16[3,1024,128]{2,1,0:T(8,128)(2,1)}, bf16[3,1024,128]{2,1,0:T(8,128)(2,1)S(1)}, u32[]{:S(2)}) copy-start(bf16[3,1024,128]{2,1,0:T(8,128)(2,1)S(1)} %get-tuple-element.6) | copy-start | bytes 2359300
  124.2 74.5 %collective-permute-start.2 = (bf16[3,768,256]{2,1,0:T(8,128)(2,1)}, bf16[3,768,256]{2,1,0:T(8,128)(2,1)S(1)}, u32[]{:S(2)}, u32[]{:S(2)}) collective-permute-start(bf16[3,768,256]{2,1,0:T(8,128)(2,1)} %get-tuple-element.12), channel_id=1, source_target_pairs={{0,8},{8,16},{16,24},{24,32},{32,40},{40,48},{48,56},{56,64},{64,7... | collective-permute-start | bytes 3538952 | tf_op jit(solution)/shard_map/ppermute | solution.py:437
  128.3 70.5 %collective-permute-start.3 = (bf16[3,768,256]{2,1,0:T(8,128)(2,1)}, bf16[3,768,256]{2,1,0:T(8,128)(2,1)}, u32[]{:S(2)}, u32[]{:S(2)}) collective-permute-start(bf16[3,768,256]{2,1,0:T(8,128)(2,1)} %get-tuple-element.13), channel_id=1, source_target_pairs={{8,0},{16,8},{24,16},{32,24},{40,32},{48,40},{56,48},{64,56},{72,6... | collective-permute-start | bytes 3538952 | tf_op jit(solution)/shard_map/ppermute | solution.py:436
  135.2 63.6 %copy-start.4 = (f32[3,1024,256]{2,1,0:T(8,128)S(1)}, f32[3,1024,256]{2,1,0:T(8,128)}, u32[]{:S(2)}) copy-start(f32[3,1024,256]{2,1,0:T(8,128)} %copy-done.3) | copy-start | bytes 9437188
  198.8 1.9 copy-start.7
  211.2 37.8 %copy-start.10 = (bf16[128,3072]{1,0:T(8,128)(2,1)S(1)}, bf16[128,3072]{1,0:T(8,128)(2,1)}, u32[]{:S(2)}) copy-start(bf16[128,3072]{1,0:T(8,128)(2,1)} %param.8) | copy-start | bytes 2359300
  211.2 37.8 %copy-start.15 = (f32[128]{0:T(128)S(1)}, f32[128]{0:T(128)}, u32[]{:S(2)}) copy-start(f32[128]{0:T(128)} %copy-done.14) | copy-start | bytes 1540
  249.1 0.7 copy-start.13

commit v3 on v2

--- a/solution.py
+++ b/solution.py
@@ -15,6 +15,7 @@
 HD = 128
 EPSILON = 1e-06
 MASKED = -1e30
+HELD = 3
 
 
 def norm_rows(inputs, mod_gain, mod_shift):
@@ -42,8 +43,7 @@
     diagonal = (offsets == RADIUS) & (query_tile == key_tile)
     allowed = ((tile_mask == 1) | diagonal) & (source >= 0) & (source < total_frames)
     bias = jnp.where(allowed, 0.0, MASKED).astype(jnp.float32)
-    bias = jnp.transpose(bias, (0, 1, 3, 2))
-    return jnp.repeat(bias, TILE, axis=3)
+    return jnp.transpose(bias, (0, 1, 3, 2)).reshape(-1)
 
 
 def dot(a, b, dims):
@@ -55,32 +55,88 @@
 
 
 def attention_kernel(
-    joined, low, high, grad_out, bias, out, grad_q, own, rims,
-    keys, values, keys_t, values_t, exps, grad_k, grad_v,
+    bias, joined, grad_out, out, grad_q, grad_pairs,
+    keys, values, keys_t, values_t, exps, grad_k, grad_v, own, halo, rims, landed,
+    halo_send, halo_recv, rims_send, rims_recv,
 ):
+    head = pl.program_id(0)
     frame = pl.program_id(1)
+    heads = pl.num_programs(0)
     frames = pl.num_programs(1)
     block = 4 * FRAME
     rim = RADIUS * FRAME
+    spare = block - rim
     scale = HD ** (-0.5)
+    me = lax.axis_index("tm")
+    count = lax.axis_size("tm")
+    above, below = lax.rem(me + 1, count), lax.rem(me + count - 1, count)
+
+    def halo_copy(which, side):
+        rows = slice(spare, block) if side == 0 else slice(0, rim)
+        return pltpu.make_async_remote_copy(
+            src_ref=joined.at[which, rows, HD : 3 * HD],
+            dst_ref=halo.at[which, side],
+            send_sem=halo_send.at[which, side],
+            recv_sem=halo_recv.at[which, side],
+            device_id={"tm": above if side == 0 else below},
+            device_id_type=pl.DeviceIdType.MESH,
+        )
+
+    def rims_copy(which, side):
+        return pltpu.make_async_remote_copy(
+            src_ref=rims.at[which, side],
+            dst_ref=landed.at[which, side],
+            send_sem=rims_send.at[which, side],
+            recv_sem=rims_recv.at[which, side],
+            device_id={"tm": above if side == 0 else below},
+            device_id_type=pl.DeviceIdType.MESH,
+        )
+
+    @pl.when((head == 0) & (frame == 0))
+    def _():
+        barrier = pltpu.get_barrier_semaphore()
+        for neighbour in (above, below):
+            pl.semaphore_signal(
+                barrier, inc=1, device_id={"tm": neighbour}, device_id_type=pl.DeviceIdType.MESH
+            )
+        pl.semaphore_wait(barrier, 2)
+        for which in range(HELD):
+            for side in range(2):
+                halo_copy(which, side).start()
 
     @pl.when(frame == 0)
     def _():
-        keys[0:rim, :] = low[0, :, 0:HD]
-        keys[rim : rim + block, :] = joined[0, :, HD : 2 * HD]
-        keys[rim + block :, :] = high[0, :, 0:HD]
-        values[0:rim, :] = low[0, :, HD:]
-        values[rim : rim + block, :] = joined[0, :, 2 * HD :]
-        values[rim + block :, :] = high[0, :, HD:]
+        keys[rim : rim + block, :] = joined[head, :, HD : 2 * HD]
+        values[rim : rim + block, :] = joined[head, :, 2 * HD :]
+        grad_k[...] = jnp.zeros_like(grad_k)
+        grad_v[...] = jnp.zeros_like(grad_v)
+        for which in range(HELD):
+
+            @pl.when(head == which)
+            def _():
+                for side in range(2):
+                    halo_copy(which, side).wait_recv()
+                keys[0:rim, :] = halo[which, 0, :, 0:HD]
+                keys[rim + block :, :] = halo[which, 1, :, 0:HD]
+                values[0:rim, :] = halo[which, 0, :, HD:]
+                values[rim + block :, :] = halo[which, 1, :, HD:]
+
         for part in range(block // FRAME + 2 * RADIUS):
             rows = slice(part * FRAME, (part + 1) * FRAME)
             keys_t[part, :, :] = keys[rows, :].T
             values_t[part, :, :] = values[rows, :].T
-        grad_k[...] = jnp.zeros_like(grad_k)
-        grad_v[...] = jnp.zeros_like(grad_v)
+
+    query_tile = lax.broadcasted_iota(jnp.int32, (1, FRAME), 1) // TILE
+
+    def bias_line(offset, tile):
+        first = (frame * SPAN + offset) * 16 + tile * 4
+        line = jnp.full((1, FRAME), bias[first], jnp.float32)
+        for other in range(1, 4):
+            line = jnp.where(query_tile == other, bias[first + other], line)
+        return line
 
     own_rows = pl.ds(pl.multiple_of(frame * FRAME, FRAME), FRAME)
-    query = joined[0, own_rows, 0:HD]
+    query = joined[head, own_rows, 0:HD]
     grads = grad_out[0, own_rows, :]
 
     totals = jnp.zeros((8, FRAME), jnp.float32)
@@ -90,7 +146,7 @@
         scores = dot(keys[rows, :], query, NT) * (scale * math.log2(math.e))
         parts = []
         for tile in range(FRAME // TILE):
-            line = bias[0, offset, tile : tile + 1, :]
+            line = bias_line(offset, tile)
             parts.append(jnp.exp2(scores[tile * TILE : (tile + 1) * TILE, :] + line))
         exponent = jnp.concatenate(parts, axis=0)
         exps[offset * FRAME : (offset + 1) * FRAME, :] = exponent
@@ -115,42 +171,58 @@
 
     @pl.when(frame == frames - 1)
     def _():
-        own[0, :, 0:HD] = grad_k[rim : rim + block, :] * scale
-        own[0, :, HD:] = grad_v[rim : rim + block, :]
-        rims[0, 0:rim, 0:HD] = (grad_k[0:rim, :] * scale).astype(jnp.bfloat16)
-        rims[0, rim:, 0:HD] = (grad_k[rim + block :, :] * scale).astype(jnp.bfloat16)
-        rims[0, 0:rim, HD:] = grad_v[0:rim, :].astype(jnp.bfloat16)
-        rims[0, rim:, HD:] = grad_v[rim + block :, :].astype(jnp.bfloat16)
-
-
-def attention(joined, low, high, grad_out, bias):
+        for which in range(HELD):
+
+            @pl.when(head == which)
+            def _():
+                own[which, :, 0:HD] = grad_k[rim : rim + block, :] * scale
+                own[which, :, HD:] = grad_v[rim : rim + block, :]
+                rims[which, 1, :, 0:HD] = (grad_k[0:rim, :] * scale).astype(jnp.bfloat16)
+                rims[which, 0, :, 0:HD] = (grad_k[rim + block :, :] * scale).astype(jnp.bfloat16)
+                rims[which, 1, :, HD:] = grad_v[0:rim, :].astype(jnp.bfloat16)
+                rims[which, 0, :, HD:] = grad_v[rim + block :, :].astype(jnp.bfloat16)
+                for side in range(2):
+                    rims_copy(which, side).start()
+
+    @pl.when((head == heads - 1) & (frame == frames - 1))
+    def _():
+        for which in range(HELD):
+            for side in range(2):
+                rims_copy(which, side).wait_recv()
+            own[which, 0:rim, :] += landed[which, 0].astype(jnp.float32)
+            own[which, spare:, :] += landed[which, 1].astype(jnp.float32)
+            grad_pairs[which, :, :] = own[which, :, :].astype(jnp.bfloat16)
+        for which in range(HELD):
+            for side in range(2):
+                halo_copy(which, side).wait_send()
+                rims_copy(which, side).wait_send()
+
+
+def attention(joined, grad_out, bias):
     heads, block, _ = joined.shape
     frames = block // FRAME
     rim = RADIUS * FRAME
     whole = block + 2 * rim
     per_head = lambda head, frame: (head, 0, 0)
     per_frame = lambda head, frame: (head, frame, 0)
+    constant = lambda head, frame: (0, 0, 0)
     return pl.pallas_call(
         attention_kernel,
         grid=(heads, frames),
         out_shape=(
             jax.ShapeDtypeStruct((heads, block, HD), jnp.bfloat16),
             jax.ShapeDtypeStruct((heads, block, HD), jnp.bfloat16),
-            jax.ShapeDtypeStruct((heads, block, 2 * HD), jnp.float32),
-            jax.ShapeDtypeStruct((heads, 2 * rim, 2 * HD), jnp.bfloat16),
+            jax.ShapeDtypeStruct((heads, block, 2 * HD), jnp.bfloat16),
         ),
         in_specs=[
-            pl.BlockSpec((1, block, 3 * HD), per_head),
-            pl.BlockSpec((1, rim, 2 * HD), per_head),
-            pl.BlockSpec((1, rim, 2 * HD), per_head),
+            pl.BlockSpec(memory_space=pltpu.SMEM),
+            pl.BlockSpec((heads, block, 3 * HD), constant),
             pl.BlockSpec((1, block, HD), per_head),
-            pl.BlockSpec((1, SPAN, 4, FRAME), lambda head, frame: (frame, 0, 0, 0)),
         ],
         out_specs=(
             pl.BlockSpec((1, FRAME, HD), per_frame),
             pl.BlockSpec((1, FRAME, HD), per_frame),
-            pl.BlockSpec((1, block, 2 * HD), per_head),
-            pl.BlockSpec((1, 2 * rim, 2 * HD), per_head),
+            pl.BlockSpec((heads, block, 2 * HD), constant),
         ),
         scratch_shapes=[
             pltpu.VMEM((whole, HD), jnp.bfloat16),
@@ -160,12 +232,23 @@
             pltpu.VMEM((SPAN * FRAME, FRAME), jnp.float32),
             pltpu.VMEM((whole, HD), jnp.float32),
             pltpu.VMEM((whole, HD), jnp.float32),
+            pltpu.VMEM((heads, block, 2 * HD), jnp.float32),
+            pltpu.VMEM((heads, 2, rim, 2 * HD), jnp.bfloat16),
+            pltpu.VMEM((heads, 2, rim, 2 * HD), jnp.bfloat16),
+            pltpu.VMEM((heads, 2, rim, 2 * HD), jnp.bfloat16),
+            pltpu.SemaphoreType.DMA((heads, 2)),
+            pltpu.SemaphoreType.DMA((heads, 2)),
+            pltpu.SemaphoreType.DMA((heads, 2)),
+            pltpu.SemaphoreType.DMA((heads, 2)),
         ],
         compiler_params=pltpu.CompilerParams(
-            dimension_semantics=("arbitrary", "arbitrary"), vmem_limit_bytes=40 << 20
+            dimension_semantics=("arbitrary", "arbitrary"),
+            collective_id=3,
+            has_side_effects=True,
+            vmem_limit_bytes=40 << 20,
         ),
         name="attention",
-    )(joined, low, high, grad_out, bias)
+    )(bias, joined, grad_out)
 
 
 SIXTH = 512
@@ -412,35 +495,21 @@
     activations, mod_gain, mod_shift, out_gate, qkv_weight, out_weight, tile_mask, cotangent
 ):
     shard_rows = activations.shape[0]
-    group_rows = cotangent.shape[0]
     frame_count = tile_mask.shape[0]
-    rim = RADIUS * FRAME
     standard, inverse, modulated = norm_rows(activations, mod_gain, mod_shift)
     rows_here = gather_rows(modulated)
     weight = jnp.transpose(qkv_weight, (1, 0, 2))
     joined = jnp.einsum("rd,hdc->hrc", rows_here, weight, preferred_element_type=jnp.float32)
     joined = joined.astype(jnp.bfloat16)
     count = lax.axis_size("tm")
-    upward = [(i, i + 1) for i in range(count - 1)]
-    downward = [(i + 1, i) for i in range(count - 1)]
-    low = lax.ppermute(joined[:, group_rows - rim :, HD:], "tm", upward)
-    high = lax.ppermute(joined[:, :rim, HD:], "tm", downward)
     scaled = (cotangent.astype(jnp.float32) * out_gate).astype(jnp.bfloat16)
     grad_out = jnp.einsum("rd,hcd->hrc", scaled, out_weight, preferred_element_type=jnp.float32)
     grad_out = grad_out.astype(jnp.bfloat16)
     bias = mask_bias(tile_mask, lax.axis_index("tm") * frame_count, frame_count * count)
-    output, grad_queries, own, rims = attention(joined, low, high, grad_out, bias)
+    output, grad_queries, grad_pairs = attention(joined, grad_out, bias)
     projected = jnp.einsum("hrc,hcd->rd", output, out_weight, preferred_element_type=jnp.float32)
     projection = scatter_rows(projected.astype(jnp.bfloat16), 1, "scatter_out")
     layer_out = (activations.astype(jnp.float32) + out_gate * projection).astype(jnp.bfloat16)
-    from_above = lax.ppermute(rims[:, :rim], "tm", downward).astype(jnp.float32)
-    from_below = lax.ppermute(rims[:, rim:], "tm", upward).astype(jnp.float32)
-    spare = group_rows - rim
-    grad_pairs = (
-        own
-        + jnp.pad(from_below, ((0, 0), (0, spare), (0, 0)))
-        + jnp.pad(from_above, ((0, 0), (spare, 0), (0, 0)))
-    ).astype(jnp.bfloat16)
     grad_joined = jnp.concatenate([grad_queries, grad_pairs], axis=-1)
     grad_rows = jnp.einsum("hrc,hdc->rd", grad_joined, weight, preferred_element_type=jnp.float32)
     grad_norm = scatter_rows(grad_rows.astype(jnp.bfloat16), 2, "scatter_grad")

time: 255 us -> 235 us (0.922)
  Pallas kernels: 177 us -> 193 us
  starting transfers between devices: 12.2 us -> 0 us
  waiting for transfers between devices: 12.1 us -> 0 us
  local copies, waits for them, and re-layouts: 10.3 us -> 2.69 us
  other arithmetic: 10.9 us -> 8.08 us
    pallas_call x1, Pallas kernels: 29.7 us -> 59.4 us  [attention(): pl.pallas_call(attention_kernel, grid=(heads, frames), out_shape=(jax.Sha...]
    pallas_call x2, Pallas kernels: 101 us -> 88 us  [scatter_rows(): pl.pallas_call(scatter_kernel, out_shape=jax.ShapeDtypeStruct((size, widt...]
    ppermute x4 -> x0, starting transfers between devices: 12.2 us -> none  [the longest x1 4.01 us: on_device(): from_below = lax.ppermute(rims[:, rim:], 'tm', upward).astype(jnp.float32)]
    ppermute x4 -> x0, waiting for transfers between devices: 12.1 us -> none  [the longest x1 12.1 us: on_device(): high = lax.ppermute(joined[:, :rim, HD:], 'tm', downward)]
    slice x2 -> x0, local copies, waits for them, and re-layouts: 3.51 us -> none  [the longest x1 1.77 us: on_device(): high = lax.ppermute(joined[:, :rim, HD:], 'tm', downward)]
  transfers between devices with their start and end apart: 4 -> 0, of which waited for: 1 -> 0; matrix products, arithmetic and copies ran while one was open for 7% -> 0% of each run, Pallas kernels for 25% -> 0%
where the time goes in v3:
time: 235 us
  Pallas kernels  193 us (82%)
  matrix products  29.6 us (13%)
  other arithmetic  8.08 us (3%)
  local copies, waits for them, and re-layouts  2.69 us (1%)
    pallas_call x2, Pallas kernels, scatter_rows(): pl.pallas_call(scatter_kernel, out_shape=jax.ShapeDtypeStruct((size, widt...  88 us
    pallas_call x1, Pallas kernels, attention(): pl.pallas_call(attention_kernel, grid=(heads, frames), out_shape=(jax.Sha...  59.4 us
    pallas_call x1, Pallas kernels, gather_rows(): pl.pallas_call(gather_kernel, out_shape=jax.ShapeDtypeStruct((8 * size, w...  45.9 us
    dot_general x1, matrix products, on_device(): jnp.einsum('hrc,hdc->rd', grad_joined, weight, preferred_element_type=jnp...  10.8 us
    dot_general x1, matrix products, on_device(): jnp.einsum('rd,hdc->hrc', rows_here, weight, preferred_element_type=jnp.f...  9.5 us
    dot_general x1, matrix products, on_device(): jnp.einsum('rd,hcd->hrc', scaled, out_weight, preferred_element_type=jnp....  5.7 us

profile of v3, /device:TPU:17, one launch (start us, length us, event | category | flops | bytes accessed | tf_op | source)
XLA Modules:
  0.0 234.5 jit_solution(14504207737276445427)
XLA Ops:
  0.6 0.0 copy-start
  0.6 0.0 copy-start.4
  0.7 0.0 copy-start.7
  0.7 0.0 copy-start.5
  0.7 1.5 convert_reduce_fusion
  2.2 1.5 fusion.30
  3.7 0.0 copy-done.4
  3.7 0.0 copy-done.7
  3.7 0.0 copy-done.5
  3.7 0.4 fusion.24.block
  4.1 0.0 copy-start.9
  4.1 45.9 %gather_rows.1 = bf16[1024,3072]{1,0:T(8,128)(2,1)S(1)} custom-call(bf16[128,3072]{1,0:T(8,128)(2,1)S(1)} %fusion.24.block), custom_call_target="tpu_custom_call" | custom-call | bytes 188743680 | tf_op jit(solution)/shard_map/gather_rows/pallas_call | solution.py:360
  50.0 0.0 copy-done.9
  50.0 0.0 copy-start.6
  50.0 0.0 copy-start.8
  50.0 9.5 %convert_bitcast_fusion.joined = bf16[3,1024,384]{2,1,0:T(8,128)(2,1)} fusion(bf16[3072,3,384]{2,0,1:T(8,128)(2,1)S(1)} %copy-done.9, bf16[1024,3072]{1,0:T(8,128)(2,1)S(1)} %gather_rows.1), kind=kOutput, calls=%fused_computation.17 | convolution fusion | flops 7248936960 | bytes 15728640 | tf_op jit(solution)/shard_map/rd,hdc->hrc/dot_general | solution.py:502
  59.5 0.0 copy-done.6
  59.5 0.1 select_bitcast_fusion
  59.6 0.2 copy.10
  59.8 0.1 reshape.30.bias
  60.0 0.0 copy-done
  60.0 0.0 copy-done.8
  60.0 0.0 copy-start.3
  60.0 5.7 %fusion.35.grad_out = bf16[3,1024,128]{2,1,0:T(8,128)(2,1)S(1)} fusion(bf16[3,128,3072]{2,1,0:T(8,128)(2,1)S(1)} %copy-done, bf16[1024,3072]{1,0:T(8,128)(2,1)} %param.15, f32[3072]{0:T(1024)S(1)} %copy-done.8), kind=kOutput, calls=%fused_computation.34 | convolution fusion | flops 2425749504 | bytes 9449472 | tf_op jit(solution)/shard_map/rd,hcd->hrc/dot_general | solution.py:506
  65.7 0.0 copy-done.3
  65.7 59.4 %attention.1 = (bf16[3,1024,128]{2,1,0:T(8,128)(2,1)S(1)}, bf16[3,1024,128]{2,1,0:T(8,128)(2,1)S(1)}, bf16[3,1024,256]{2,1,0:T(8,128)(2,1)S(1)}) custom-call(f32[448]{0:T(512)S(1)} %reshape.30.bias, bf16[3,1024,384]{2,1,0:T(8,128)(2,1)S(1)} %copy-done.3, bf16[3,1024,128]{2,1,0:T(8,128)(2,1)S(1)} %fusion.35.grad_out), custom_call_target="tpu_custom_call" | custom-call | tf_op jit(solution)/shard_map/attention/pallas_call | solution.py:209
  125.1 10.8 %bitcast_convert_fusion.partial = bf16[1024,3072]{1,0:T(8,128)(2,1)S(1)} fusion(bf16[3072,3,384]{2,0,1:T(8,128)(2,1)} %param.12, bf16[3,1024,256]{2,1,0:T(8,128)(2,1)S(1)} %get-tuple-element.7, bf16[3,1024,128]{2,1,0:T(8,128)(2,1)S(1)} %get-tuple-element.6), kind=kOutput, calls=%fused_computation | convolution fusion | flops 7255621632 | bytes 15728640 | tf_op jit(solution)/shard_map/hrc,hdc->rd/dot_general | solution.py:514
  135.9 44.0 %scatter_grad.1 = f32[128,3072]{1,0:T(8,128)S(1)} custom-call(bf16[1024,3072]{1,0:T(8,128)(2,1)S(1)} %bitcast_convert_fusion.partial), custom_call_target="tpu_custom_call" | custom-call | bytes 188743680 | tf_op jit(solution)/shard_map/scatter_grad/pallas_call | solution.py:473
  179.9 0.0 copy-start.1
  179.9 1.2 copy-done.1
  181.1 0.5 multiply_reduce_fusion
  181.6 3.7 %bitcast_convert_fusion.1.partial = bf16[1024,3072]{1,0:T(8,128)(2,1)S(1)} fusion(bf16[3,1024,128]{2,1,0:T(8,128)(2,1)S(1)} %get-tuple-element.5, bf16[3,128,3072]{2,1,0:T(8,128)(2,1)S(1)} %copy-done), kind=kOutput, calls=%fused_computation.1 | convolution fusion | flops 2419064832 | bytes 9437184 | tf_op jit(solution)/shard_map/hrc,hcd->rd/dot_general | solution.py:510
  185.2 44.0 %scatter_out.1 = f32[128,3072]{1,0:T(8,128)S(1)} custom-call(bf16[1024,3072]{1,0:T(8,128)(2,1)S(1)} %bitcast_convert_fusion.1.partial), custom_call_target="tpu_custom_call" | custom-call | bytes 188743680 | tf_op jit(solution)/shard_map/scatter_out/pallas_call | solution.py:473
  229.2 0.0 copy-start.2
  229.2 1.2 copy-done.2
  230.4 4.1 %fusion.29 = (bf16[128,3072]{1,0:T(8,128)(2,1)}, bf16[128,3072]{1,0:T(8,128)(2,1)}) fusion(bf16[128,3072]{1,0:T(8,128)(2,1)S(1)} %copy-done.4, f32[128,3072]{1,0:T(8,128)} %copy-done.1, f32[128]{0:T(128)S(1)} %get-tuple-element.12, f32[128]{0:T(128)S(1)} %get-tuple-element.13, bf16[1024,3072]{1,0:T(8,128)(2,1)} %param.15, s32[]{:T(128)S(6)} %select_n.8, ...), kind=kLoop, calls=%fused_computation.29 | loop fusion | flops 5505024 | bytes 6318084 | tf_op jit(solution)/shard_map/convert_element_type | solution.py:34
  (5 shorter events, 0.0 us)
Async XLA Ops:
  0.6 59.3 %copy-start = (bf16[3,128,3072]{2,1,0:T(8,128)(2,1)S(1)}, bf16[3,128,3072]{2,1,0:T(8,128)(2,1)}, u32[]{:S(2)}) copy-start(bf16[3,128,3072]{2,1,0:T(8,128)(2,1)} %param.13) | copy-start | bytes 7077892
  0.6 3.0 %copy-start.4 = (bf16[128,3072]{1,0:T(8,128)(2,1)S(1)}, bf16[128,3072]{1,0:T(8,128)(2,1)}, u32[]{:S(2)}) copy-start(bf16[128,3072]{1,0:T(8,128)(2,1)} %param.8) | copy-start | bytes 2359300
  0.7 3.0 %copy-start.7 = (f32[3072]{0:T(1024)S(1)}, f32[3072]{0:T(1024)}, u32[]{:S(2)}) copy-start(f32[3072]{0:T(1024)} %param.10) | copy-start | bytes 36868
  0.7 3.0 %copy-start.5 = (f32[3072]{0:T(1024)S(1)}, f32[3072]{0:T(1024)}, u32[]{:S(2)}) copy-start(f32[3072]{0:T(1024)} %param.9) | copy-start | bytes 36868
  4.1 45.9 %copy-start.9 = (bf16[3072,3,384]{2,0,1:T(8,128)(2,1)S(1)}, bf16[3072,3,384]{2,0,1:T(8,128)(2,1)}, u32[]{:S(2)}) copy-start(bf16[3072,3,384]{2,0,1:T(8,128)(2,1)} %param.12) | copy-start | bytes 21233668
  50.0 9.5 %copy-start.6 = (s32[4,7,4,4]{1,3,2,0:T(4,128)S(1)}, s32[4,7,4,4]{1,3,2,0:T(4,128)}, u32[]{:S(2)}) copy-start(s32[4,7,4,4]{1,3,2,0:T(4,128)} %param.14) | copy-start | bytes 5380
  50.0 10.0 %copy-start.8 = (f32[3072]{0:T(1024)S(1)}, f32[3072]{0:T(1024)}, u32[]{:S(2)}) copy-start(f32[3072]{0:T(1024)} %param.11) | copy-start | bytes 36868
  60.0 5.7 %copy-start.3 = (bf16[3,1024,384]{2,1,0:T(8,128)(2,1)S(1)}, bf16[3,1024,384]{2,1,0:T(8,128)(2,1)}, u32[]{:S(2)}) copy-start(bf16[3,1024,384]{2,1,0:T(8,128)(2,1)} %convert_bitcast_fusion.joined) | copy-start | bytes 7077892
  179.9 1.2 copy-start.1
  229.2 1.2 copy-start.2

commit v4 on v3

--- a/solution.py
+++ b/solution.py
@@ -279,7 +279,16 @@
     pl.semaphore_wait(barrier, len(neighbours))
 
 
-def gather_kernel(block, out, send, recv, own_sem):
+def gather_kernel(
+    gate, block, cotangent, weight, out_weight, joined, grad_out,
+    out, held_cotangent, held_weight, held_out_weight, send, recv, own_sem, loads,
+):
+    fetches = []
+    for number, (source, target) in enumerate(
+        ((cotangent, held_cotangent), (out_weight, held_out_weight), (weight, held_weight))
+    ):
+        fetches.append(pltpu.make_async_copy(source, target, loads.at[number]))
+        fetches[-1].start()
     place = ring_places()
     up, down, across = place(0, 1), place(0, -1), place(1, 0)
     size = block.shape[0]
@@ -326,6 +335,23 @@
     push(11, across, block, 0, 0, LOW)
     own = pltpu.make_async_copy(block, out.at[rows(0, 0), :], own_sem)
     own.start()
+    fetches[0].wait()
+    fetches[1].wait()
+
+    def grad_rows(step, carry):
+        chunk = pl.ds(pl.multiple_of(step * FRAME, FRAME), FRAME)
+        scaled = (held_cotangent[chunk, :].astype(jnp.float32) * gate[...]).astype(jnp.bfloat16)
+        for head in range(HELD):
+            grad_out[head, chunk, :] = dot(scaled, held_out_weight[head], NT).astype(jnp.bfloat16)
+        return carry
+
+    lax.fori_loop(0, 8 * size // FRAME, grad_rows, 0)
+
+    def join(other, shift):
+        for head in range(HELD):
+            product = dot(out[rows(other, shift), :], held_weight[head], NN)
+            joined[head, rows(other, shift), :] = product.astype(jnp.bfloat16)
+
     arrived(0, 0, -1, LOW)
     push(2, up, None, 0, -1, LOW)
     push(12, across, None, 0, -1, LOW)
@@ -334,8 +360,16 @@
     arrived(10, 1, 0, HIGH)
     push(3, up, None, 1, 0, HIGH)
     push(8, down, None, 1, 0, HIGH)
+    own.wait()
+    fetches[2].wait()
+    join(0, 0)
     arrived(6, 0, 1, LOW)
     push(13, across, None, 0, 1, LOW)
+    arrived(1, 0, -1, HIGH)
+    join(0, -1)
+    join(0, 1)
+    arrived(11, 1, 0, LOW)
+    join(1, 0)
     arrived(12, 1, -1, LOW)
     push(4, up, None, 1, -1, (0, 2))
     arrived(7, 0, 2, HIGH)
@@ -343,38 +377,46 @@
     arrived(13, 1, 1, LOW)
     arrived(8, 1, 1, HIGH)
     push(9, down, None, 1, 1, (2, 4))
-    arrived(1, 0, -1, HIGH)
-    arrived(11, 1, 0, LOW)
+    join(1, 1)
     arrived(2, 0, 2, LOW)
+    join(0, 2)
     arrived(3, 1, -1, HIGH)
+    join(1, -1)
     arrived(4, 1, 2, (0, 2))
     arrived(9, 1, 2, (2, 4))
     arrived(14, 1, 2, (4, 6))
+    join(1, 2)
     for copy in started:
         copy.wait_send()
-    own.wait()
-
-
-def gather_rows(block):
+
+
+def gather_rows(gate, block, cotangent, weight, out_weight):
     size, width = block.shape
+    in_vmem = pl.BlockSpec(memory_space=pltpu.VMEM)
+    anywhere = pl.BlockSpec(memory_space=pl.ANY)
     return pl.pallas_call(
         gather_kernel,
-        out_shape=jax.ShapeDtypeStruct((8 * size, width), block.dtype),
-        in_specs=[pl.BlockSpec(memory_space=pltpu.VMEM)],
-        out_specs=pl.BlockSpec(memory_space=pltpu.VMEM),
+        out_shape=(
+            jax.ShapeDtypeStruct((HELD, 8 * size, 3 * HD), block.dtype),
+            jax.ShapeDtypeStruct((HELD, 8 * size, HD), block.dtype),
+        ),
+        in_specs=[in_vmem, in_vmem, anywhere, anywhere, anywhere],
+        out_specs=(in_vmem, in_vmem),
         scratch_shapes=[
+            pltpu.VMEM((8 * size, width), block.dtype),
+            pltpu.VMEM(cotangent.shape, cotangent.dtype),
+            pltpu.VMEM(weight.shape, weight.dtype),
+            pltpu.VMEM(out_weight.shape, out_weight.dtype),
             pltpu.SemaphoreType.DMA((15,)),
             pltpu.SemaphoreType.DMA((15,)),
             pltpu.SemaphoreType.DMA(()),
+            pltpu.SemaphoreType.DMA((3,)),
         ],
         compiler_params=pltpu.CompilerParams(
-            collective_id=0, has_side_effects=True, vmem_limit_bytes=40 << 20
-        ),
-        cost_estimate=pl.CostEstimate(
-            flops=0, bytes_accessed=180 << 20, transcendentals=0
+            collective_id=0, has_side_effects=True, vmem_limit_bytes=48 << 20
         ),
         name="gather_rows",
-    )(block)
+    )(gate.reshape(1, width), block, cotangent, weight, out_weight)
 
 
 def scatter_kernel(partial, out, landing, staged, send, recv):
@@ -497,14 +539,9 @@
     shard_rows = activations.shape[0]
     frame_count = tile_mask.shape[0]
     standard, inverse, modulated = norm_rows(activations, mod_gain, mod_shift)
-    rows_here = gather_rows(modulated)
     weight = jnp.transpose(qkv_weight, (1, 0, 2))
-    joined = jnp.einsum("rd,hdc->hrc", rows_here, weight, preferred_element_type=jnp.float32)
-    joined = joined.astype(jnp.bfloat16)
+    joined, grad_out = gather_rows(out_gate, modulated, cotangent, weight, out_weight)
     count = lax.axis_size("tm")
-    scaled = (cotangent.astype(jnp.float32) * out_gate).astype(jnp.bfloat16)
-    grad_out = jnp.einsum("rd,hcd->hrc", scaled, out_weight, preferred_element_type=jnp.float32)
-    grad_out = grad_out.astype(jnp.bfloat16)
     bias = mask_bias(tile_mask, lax.axis_index("tm") * frame_count, frame_count * count)
     output, grad_queries, grad_pairs = attention(joined, grad_out, bias)
     projected = jnp.einsum("hrc,hcd->rd", output, out_weight, preferred_element_type=jnp.float32)

time: 235 us -> 220 us (0.936)
  matrix products: 29.6 us -> 14.2 us
    dot_general x2 -> x0, matrix products: 15.2 us -> none  [the longest x1 9.5 us: on_device(): jnp.einsum('rd,hdc->hrc', rows_here, weight, preferred_element_type=jnp.f...]
where the time goes in v4:
time: 220 us; the launch traced here: 219 us
  Pallas kernels  195 us (89%)
  matrix products  14.2 us (6%)
  other arithmetic  7.36 us (3%)
    pallas_call x2, Pallas kernels, scatter_rows(): pl.pallas_call(scatter_kernel, out_shape=jax.ShapeDtypeStruct((size, widt...  88.1 us
    pallas_call x1, Pallas kernels, attention(): pl.pallas_call(attention_kernel, grid=(heads, frames), out_shape=(jax.Sha...  59.9 us
    pallas_call x1, Pallas kernels, gather_rows(): pl.pallas_call(gather_kernel, out_shape=(jax.ShapeDtypeStruct((HELD, 8 *...  47.4 us
    dot_general x1, matrix products, on_device(): jnp.einsum('hrc,hdc->rd', grad_joined, weight, preferred_element_type=jnp...  10.6 us

profile of v4, /device:TPU:17, one launch (start us, length us, event | category | flops | bytes accessed | tf_op | source)
XLA Modules:
  0.0 219.4 jit_solution(8034213634409222797)
XLA Ops:
  0.6 0.0 copy-start.1
  0.6 0.0 copy-start.6
  0.7 0.0 copy-start.4
  0.7 0.0 copy-start
  0.7 1.4 convert_reduce_fusion
  2.1 1.5 fusion.15
  3.6 0.0 copy-done.1
  3.6 0.0 copy-done.6
  3.6 0.0 copy-done.4
  3.6 0.4 fusion.9.block
  4.0 0.0 copy-done
  4.0 0.0 copy-start.5
  4.0 47.4 %gather_rows.1 = (bf16[3,1024,384]{2,1,0:T(8,128)(2,1)S(1)}, bf16[3,1024,128]{2,1,0:T(8,128)(2,1)S(1)}) custom-call(f32[1,3072]{1,0:T(1,128)S(1)} %bitcast.12, bf16[128,3072]{1,0:T(8,128)(2,1)S(1)} %fusion.9.block, bf16[1024,3072]{1,0:T(8,128)(2,1)} %cotangent.1, bf16[3,3072,384]{2,1,0:T(8,128)(2,1)} %bitcast.13, bf16[3,128,3072]{2,1,0:T(8,128)(2,1)} %out_weight.1), custom_call_target="tpu_custom_call" | custom-call | tf_op jit(solution)/shard_map/gather_rows/pallas_call | solution.py:397
  51.5 0.0 copy-done.5
  51.5 0.1 select_bitcast_fusion
  51.6 0.2 copy.10
  51.8 0.1 reshape.31.bias
  51.9 59.9 %attention.1 = (bf16[3,1024,128]{2,1,0:T(8,128)(2,1)S(1)}, bf16[3,1024,128]{2,1,0:T(8,128)(2,1)S(1)}, bf16[3,1024,256]{2,1,0:T(8,128)(2,1)S(1)}) custom-call(f32[448]{0:T(512)S(1)} %reshape.31.bias, bf16[3,1024,384]{2,1,0:T(8,128)(2,1)S(1)} %get-tuple-element.7.joined, bf16[3,1024,128]{2,1,0:T(8,128)(2,1)S(1)} %get-tuple-element.8.grad_out), custom_call_target="tpu_custom_call" | custom-call | tf_op jit(solution)/shard_map/attention/pallas_call | solution.py:209
  111.8 10.6 %bitcast_convert_fusion.partial = bf16[1024,3072]{1,0:T(8,128)(2,1)S(1)} fusion(bf16[3,1024,256]{2,1,0:T(8,128)(2,1)S(1)} %get-tuple-element.11, bf16[3,1024,128]{2,1,0:T(8,128)(2,1)S(1)} %get-tuple-element.10, bf16[3072,3,384]{2,0,1:T(8,128)(2,1)} %param.12), kind=kOutput, calls=%fused_computation | convolution fusion | flops 7255621632 | bytes 15728640 | tf_op jit(solution)/shard_map/hrc,hdc->rd/dot_general | solution.py:551
  122.4 0.0 copy-start.2
  122.4 44.0 %scatter_grad.1 = f32[128,3072]{1,0:T(8,128)S(1)} custom-call(bf16[1024,3072]{1,0:T(8,128)(2,1)S(1)} %bitcast_convert_fusion.partial), custom_call_target="tpu_custom_call" | custom-call | bytes 188743680 | tf_op jit(solution)/shard_map/scatter_grad/pallas_call | solution.py:515
  166.5 0.0 copy-done.2
  166.5 0.0 copy-start.3
  166.5 0.5 multiply_reduce_fusion
  167.0 1.1 copy-done.3
  168.1 3.6 %bitcast_convert_fusion.1.partial = bf16[1024,3072]{1,0:T(8,128)(2,1)S(1)} fusion(bf16[3,1024,128]{2,1,0:T(8,128)(2,1)S(1)} %get-tuple-element.9, bf16[3,128,3072]{2,1,0:T(8,128)(2,1)S(1)} %copy-done.3), kind=kOutput, calls=%fused_computation.1 | convolution fusion | flops 2419064832 | bytes 9437184 | tf_op jit(solution)/shard_map/hrc,hcd->rd/dot_general | solution.py:547
  171.8 44.1 %scatter_out.1 = f32[128,3072]{1,0:T(8,128)S(1)} custom-call(bf16[1024,3072]{1,0:T(8,128)(2,1)S(1)} %bitcast_convert_fusion.1.partial), custom_call_target="tpu_custom_call" | custom-call | bytes 188743680 | tf_op jit(solution)/shard_map/scatter_out/pallas_call | solution.py:515
  215.9 3.5 %fusion.14 = (bf16[128,3072]{1,0:T(8,128)(2,1)}, bf16[128,3072]{1,0:T(8,128)(2,1)}) fusion(bf16[128,3072]{1,0:T(8,128)(2,1)} %param.8, f32[128,3072]{1,0:T(8,128)S(1)} %scatter_grad.1, f32[128]{0:T(128)S(1)} %get-tuple-element.16, f32[128]{0:T(128)S(1)} %get-tuple-element.17, bf16[1024,3072]{1,0:T(8,128)(2,1)} %cotangent.1, s32[]{:T(128)S(6)} %select_n.8, ...), kind=kLoop, calls=%fused_computation.19 | loop fusion | flops 5505024 | bytes 6318084 | tf_op jit(solution)/shard_map/convert_element_type | solution.py:34
  (5 shorter events, 0.0 us)
Async XLA Ops:
  0.6 2.9 %copy-start.1 = (bf16[128,3072]{1,0:T(8,128)(2,1)S(1)}, bf16[128,3072]{1,0:T(8,128)(2,1)}, u32[]{:S(2)}) copy-start(bf16[128,3072]{1,0:T(8,128)(2,1)} %param.8) | copy-start | bytes 2359300
  0.6 2.9 %copy-start.6 = (f32[3072]{0:T(1024)S(1)}, f32[3072]{0:T(1024)}, u32[]{:S(2)}) copy-start(f32[3072]{0:T(1024)} %param.10) | copy-start | bytes 36868
  0.7 2.9 %copy-start.4 = (f32[3072]{0:T(1024)S(1)}, f32[3072]{0:T(1024)}, u32[]{:S(2)}) copy-start(f32[3072]{0:T(1024)} %param.9) | copy-start | bytes 36868
  0.7 3.3 %copy-start = (f32[3072]{0:T(1024)S(1)}, f32[3072]{0:T(1024)}, u32[]{:S(2)}) copy-start(f32[3072]{0:T(1024)} %param.11) | copy-start | bytes 36868
  4.0 47.5 %copy-start.5 = (s32[4,7,4,4]{1,3,2,0:T(4,128)S(1)}, s32[4,7,4,4]{1,3,2,0:T(4,128)}, u32[]{:S(2)}) copy-start(s32[4,7,4,4]{1,3,2,0:T(4,128)} %param.14) | copy-start | bytes 5380
  122.4 44.0 %copy-start.2 = (bf16[128,3072]{1,0:T(8,128)(2,1)S(1)}, bf16[128,3072]{1,0:T(8,128)(2,1)}, u32[]{:S(2)}) copy-start(bf16[128,3072]{1,0:T(8,128)(2,1)} %param.8) | copy-start | bytes 2359300
  166.5 1.7 copy-start.3

commit v5 on v4

--- a/solution.py
+++ b/solution.py
@@ -55,7 +55,7 @@
 
 
 def attention_kernel(
-    bias, joined, grad_out, out, grad_q, grad_pairs,
+    bias, joined, grad_out, out_weight, projected, grad_q, grad_pairs, out,
     keys, values, keys_t, values_t, exps, grad_k, grad_v, own, halo, rims, landed,
     halo_send, halo_recv, rims_send, rims_recv,
 ):
@@ -154,7 +154,7 @@
         numer += dot(values_t[frame + offset], exponent.astype(jnp.bfloat16), NN)
     inverse = 1.0 / jnp.sum(totals, axis=0, keepdims=True)
     output = (numer * inverse).T.astype(jnp.bfloat16)
-    out[0] = output
+    out[head, own_rows, :] = output
     product = grads.astype(jnp.float32) * output.astype(jnp.float32)
     delta = jnp.sum(product.T, axis=0, keepdims=True)
 
@@ -186,6 +186,13 @@
 
     @pl.when((head == heads - 1) & (frame == frames - 1))
     def _():
+        def project(step, carry):
+            chunk = pl.ds(pl.multiple_of(step * FRAME, FRAME), FRAME)
+            joint = jnp.concatenate([out[which, chunk, :] for which in range(HELD)], axis=1)
+            projected[chunk, :] = dot(joint, out_weight[...], NN).astype(jnp.bfloat16)
+            return carry
+
+        lax.fori_loop(0, block // FRAME, project, 0)
         for which in range(HELD):
             for side in range(2):
                 rims_copy(which, side).wait_recv()
@@ -198,7 +205,7 @@
                 rims_copy(which, side).wait_send()
 
 
-def attention(joined, grad_out, bias):
+def attention(joined, grad_out, bias, out_weight):
     heads, block, _ = joined.shape
     frames = block // FRAME
     rim = RADIUS * FRAME
@@ -210,7 +217,7 @@
         attention_kernel,
         grid=(heads, frames),
         out_shape=(
-            jax.ShapeDtypeStruct((heads, block, HD), jnp.bfloat16),
+            jax.ShapeDtypeStruct((block, out_weight.shape[1]), jnp.bfloat16),
             jax.ShapeDtypeStruct((heads, block, HD), jnp.bfloat16),
             jax.ShapeDtypeStruct((heads, block, 2 * HD), jnp.bfloat16),
         ),
@@ -218,13 +225,15 @@
             pl.BlockSpec(memory_space=pltpu.SMEM),
             pl.BlockSpec((heads, block, 3 * HD), constant),
             pl.BlockSpec((1, block, HD), per_head),
+            pl.BlockSpec(out_weight.shape, lambda head, frame: (0, 0)),
         ],
         out_specs=(
-            pl.BlockSpec((1, FRAME, HD), per_frame),
+            pl.BlockSpec((block, out_weight.shape[1]), lambda head, frame: (0, 0)),
             pl.BlockSpec((1, FRAME, HD), per_frame),
             pl.BlockSpec((heads, block, 2 * HD), constant),
         ),
         scratch_shapes=[
+            pltpu.VMEM((heads, block, HD), jnp.bfloat16),
             pltpu.VMEM((whole, HD), jnp.bfloat16),
             pltpu.VMEM((whole, HD), jnp.bfloat16),
             pltpu.VMEM((whole // FRAME, HD, FRAME), jnp.bfloat16),
@@ -245,10 +254,10 @@
             dimension_semantics=("arbitrary", "arbitrary"),
             collective_id=3,
             has_side_effects=True,
-            vmem_limit_bytes=40 << 20,
+            vmem_limit_bytes=56 << 20,
         ),
         name="attention",
-    )(bias, joined, grad_out)
+    )(bias, joined, grad_out, out_weight)
 
 
 SIXTH = 512
@@ -543,9 +552,10 @@
     joined, grad_out = gather_rows(out_gate, modulated, cotangent, weight, out_weight)
     count = lax.axis_size("tm")
     bias = mask_bias(tile_mask, lax.axis_index("tm") * frame_count, frame_count * count)
-    output, grad_queries, grad_pairs = attention(joined, grad_out, bias)
-    projected = jnp.einsum("hrc,hcd->rd", output, out_weight, preferred_element_type=jnp.float32)
-    projection = scatter_rows(projected.astype(jnp.bfloat16), 1, "scatter_out")
+    projected, grad_queries, grad_pairs = attention(
+        joined, grad_out, bias, out_weight.reshape(-1, out_weight.shape[2])
+    )
+    projection = scatter_rows(projected, 1, "scatter_out")
     layer_out = (activations.astype(jnp.float32) + out_gate * projection).astype(jnp.bfloat16)
     grad_joined = jnp.concatenate([grad_queries, grad_pairs], axis=-1)
     grad_rows = jnp.einsum("hrc,hdc->rd", grad_joined, weight, preferred_element_type=jnp.float32)

time: 220 us -> 224 us (1.018)
  local copies, waits for them, and re-layouts: 1.51 us -> 6.03 us
  Pallas kernels: 195 us -> 199 us
  matrix products: 14.2 us -> 10.6 us
    pallas_call x1, Pallas kernels: 59.9 us -> 64.9 us  [attention(): pl.pallas_call(attention_kernel, grid=(heads, frames), out_shape=(jax.Sha...]
    unnamed x14 -> x20, local copies, waits for them, and re-layouts: 1.18 us -> 5.12 us
    dot_general x1 -> x0, matrix products: 3.62 us -> none  [on_device(): jnp.einsum('hrc,hcd->rd', output, out_weight, preferred_element_type=jnp....]
where the time goes in v5:
time: 224 us
  Pallas kernels  199 us (89%)
  matrix products  10.6 us (5%)
  other arithmetic  7.04 us (3%)
  local copies, waits for them, and re-layouts  6.03 us (3%)
    pallas_call x2, Pallas kernels, scatter_rows(): pl.pallas_call(scatter_kernel, out_shape=jax.ShapeDtypeStruct((size, widt...  86.8 us
    pallas_call x1, Pallas kernels, attention(): pl.pallas_call(attention_kernel, grid=(heads, frames), out_shape=(jax.Sha...  64.9 us
    pallas_call x1, Pallas kernels, gather_rows(): pl.pallas_call(gather_kernel, out_shape=(jax.ShapeDtypeStruct((HELD, 8 *...  47.4 us
    dot_general x1, matrix products, on_device(): jnp.einsum('hrc,hdc->rd', grad_joined, weight, preferred_element_type=jnp...  10.6 us
    unnamed x20, local copies, waits for them, and re-layouts  5.12 us

profile of v5, /device:TPU:17, one launch (start us, length us, event | category | flops | bytes accessed | tf_op | source)
XLA Modules:
  0.0 223.5 jit_solution(9759208226560463569)
XLA Ops:
  0.6 0.0 copy-start.4
  0.6 0.0 copy-start.5
  0.7 0.0 copy-start.6
  0.7 0.0 copy-start.7
  0.7 0.0 copy-start.3
  0.7 1.4 convert_reduce_fusion
  2.1 1.5 fusion.15
  3.6 0.0 copy-done.6
  3.6 0.1 select_bitcast_fusion
  3.7 0.2 copy.10
  3.9 0.7 reshape.34.bias
  4.6 0.0 copy-done.4
  4.6 0.0 copy-done.5
  4.6 0.0 copy-done.7
  4.6 0.4 fusion.9.block
  5.0 0.0 copy-done.3
  5.0 47.4 %gather_rows.1 = (bf16[3,1024,384]{2,1,0:T(8,128)(2,1)S(1)}, bf16[3,1024,128]{2,1,0:T(8,128)(2,1)S(1)}) custom-call(f32[1,3072]{1,0:T(1,128)S(1)} %bitcast.9, bf16[128,3072]{1,0:T(8,128)(2,1)S(1)} %fusion.9.block, bf16[1024,3072]{1,0:T(8,128)(2,1)} %cotangent.1, bf16[3,3072,384]{2,1,0:T(8,128)(2,1)} %bitcast.11, bf16[3,128,3072]{2,1,0:T(8,128)(2,1)} %out_weight.1), custom_call_target="tpu_custom_call" | custom-call | tf_op jit(solution)/shard_map/gather_rows/pallas_call | solution.py:406
  52.4 0.0 copy-start.1
  52.4 1.4 copy-done.1
  53.8 0.0 copy-start.2
  53.8 0.9 copy-done.2
  54.7 64.9 %attention.1 = (bf16[1024,3072]{1,0:T(8,128)(2,1)}, bf16[3,1024,128]{2,1,0:T(8,128)(2,1)}, bf16[3,1024,256]{2,1,0:T(8,128)(2,1)}) custom-call(f32[448]{0:T(512)} %reshape.34.bias, bf16[3,1024,384]{2,1,0:T(8,128)(2,1)} %copy-done.1, bf16[3,1024,128]{2,1,0:T(8,128)(2,1)} %copy-done.2, bf16[384,3072]{1,0:T(8,128)(2,1)} %bitcast.10), custom_call_target="tpu_custom_call" | custom-call | tf_op jit(solution)/shard_map/attention/pallas_call | solution.py:216
  119.6 0.0 copy-start
  119.6 2.8 %copy-done = bf16[1024,3072]{1,0:T(8,128)(2,1)S(1)} copy-done((bf16[1024,3072]{1,0:T(8,128)(2,1)S(1)}, bf16[1024,3072]{1,0:T(8,128)(2,1)}, u32[]{:S(2)}) %copy-start) | copy-done | bytes 6291480
  122.4 0.0 copy-start.8
  122.4 0.0 copy-start.9
  122.4 43.6 %scatter_out.1 = f32[128,3072]{1,0:T(8,128)S(1)} custom-call(bf16[1024,3072]{1,0:T(8,128)(2,1)S(1)} %copy-done), custom_call_target="tpu_custom_call" | custom-call | bytes 188743680 | tf_op jit(solution)/shard_map/scatter_out/pallas_call | solution.py:524
  166.1 0.0 copy-done.8
  166.1 0.0 copy-done.9
  166.1 10.6 %bitcast_convert_fusion.partial = bf16[1024,3072]{1,0:T(8,128)(2,1)S(1)} fusion(bf16[3,1024,256]{2,1,0:T(8,128)(2,1)S(1)} %copy-done.8, bf16[3,1024,128]{2,1,0:T(8,128)(2,1)S(1)} %copy-done.9, bf16[3072,3,384]{2,0,1:T(8,128)(2,1)} %param.12), kind=kOutput, calls=%fused_computation | convolution fusion | flops 7255621632 | bytes 15728640 | tf_op jit(solution)/shard_map/hrc,hdc->rd/dot_general | solution.py:561
  176.7 43.2 %scatter_grad.1 = f32[128,3072]{1,0:T(8,128)S(1)} custom-call(bf16[1024,3072]{1,0:T(8,128)(2,1)S(1)} %bitcast_convert_fusion.partial), custom_call_target="tpu_custom_call" | custom-call | bytes 188743680 | tf_op jit(solution)/shard_map/scatter_grad/pallas_call | solution.py:524
  219.8 0.5 multiply_reduce_fusion
  220.3 3.2 %fusion.14 = (bf16[128,3072]{1,0:T(8,128)(2,1)}, bf16[128,3072]{1,0:T(8,128)(2,1)}) fusion(bf16[128,3072]{1,0:T(8,128)(2,1)S(1)} %copy-done.4, f32[128,3072]{1,0:T(8,128)S(1)} %scatter_grad.1, f32[128]{0:T(128)S(1)} %get-tuple-element.16, f32[128]{0:T(128)S(1)} %get-tuple-element.17, bf16[1024,3072]{1,0:T(8,128)(2,1)} %cotangent.1, s32[]{:T(128)S(6)} %select_n.8, ...), kind=kLoop, calls=%fused_computation.18 | loop fusion | flops 5505024 | bytes 6318084 | tf_op jit(solution)/shard_map/convert_element_type | solution.py:34
  (5 shorter events, 0.0 us)
Async XLA Ops:
  0.6 4.0 %copy-start.4 = (bf16[128,3072]{1,0:T(8,128)(2,1)S(1)}, bf16[128,3072]{1,0:T(8,128)(2,1)}, u32[]{:S(2)}) copy-start(bf16[128,3072]{1,0:T(8,128)(2,1)} %param.8) | copy-start | bytes 2359300
  0.6 4.0 %copy-start.5 = (f32[3072]{0:T(1024)S(1)}, f32[3072]{0:T(1024)}, u32[]{:S(2)}) copy-start(f32[3072]{0:T(1024)} %param.9) | copy-start | bytes 36868
  0.7 3.0 %copy-start.6 = (s32[4,7,4,4]{1,3,2,0:T(4,128)S(1)}, s32[4,7,4,4]{1,3,2,0:T(4,128)}, u32[]{:S(2)}) copy-start(s32[4,7,4,4]{1,3,2,0:T(4,128)} %param.14) | copy-start | bytes 5380
  0.7 4.0 %copy-start.7 = (f32[3072]{0:T(1024)S(1)}, f32[3072]{0:T(1024)}, u32[]{:S(2)}) copy-start(f32[3072]{0:T(1024)} %param.10) | copy-start | bytes 36868
  0.7 4.3 %copy-start.3 = (f32[3072]{0:T(1024)S(1)}, f32[3072]{0:T(1024)}, u32[]{:S(2)}) copy-start(f32[3072]{0:T(1024)} %param.11) | copy-start | bytes 36868
  52.4 1.4 copy-start.1
  53.8 0.9 copy-start.2
  119.6 2.8 %copy-start = (bf16[1024,3072]{1,0:T(8,128)(2,1)S(1)}, bf16[1024,3072]{1,0:T(8,128)(2,1)}, u32[]{:S(2)}) copy-start(bf16[1024,3072]{1,0:T(8,128)(2,1)} %get-tuple-element.9.partial) | copy-start | bytes 18874372
  122.4 43.6 %copy-start.8 = (bf16[3,1024,256]{2,1,0:T(8,128)(2,1)S(1)}, bf16[3,1024,256]{2,1,0:T(8,128)(2,1)}, u32[]{:S(2)}) copy-start(bf16[3,1024,256]{2,1,0:T(8,128)(2,1)} %get-tuple-element.11) | copy-start | bytes 4718596
  122.4 43.6 %copy-start.9 = (bf16[3,1024,128]{2,1,0:T(8,128)(2,1)S(1)}, bf16[3,1024,128]{2,1,0:T(8,128)(2,1)}, u32[]{:S(2)}) copy-start(bf16[3,1024,128]{2,1,0:T(8,128)(2,1)} %get-tuple-element.10) | copy-start | bytes 2359300
